TPU v7x, 256 devices: a whole 4x4x8 slice. The times are simulated.
256 devices in a mesh: circ: 64 (over z, y_hi, x), ax: 4 (over y_lo, core).
Axes of the slice: x: 4, y: 4 (y_hi: 2, y_lo: 2; y = y_hi * 2 + y_lo), z: 8, core: 2. Of those that a mesh axis runs over, the one named last changes fastest.
Arguments:
- fields: float32 [3, 8, 512, 1024], P(None, None, 'circ', 'ax'), may hold values from -6 to 6
Outputs:
- deriv_circ: float32 [3, 8, 512, 1024], P(None, None, 'circ', 'ax')
- deriv_axial: float32 [3, 8, 512, 1024], P(None, None, 'circ', 'ax')
- filtered: float32 [3, 8, 512, 1024], P(None, None, 'circ', 'ax')
All inputs are finite; a program needn't handle non-finite values.
Results may differ from a plain program's by a relative error of at most 0.0003.
Values sent between devices are 32-bit elements; how exact they have to be, the bound alone decides.
No kernel may reach another device: no remote copies, remote signals or barrier semaphores. Data moves between devices by JAX's collectives and lax.ppermute only.
A program may use at most 64 MiB of HBM per device.

v0:
```python
import math

import jax
import jax.numpy as jnp
import numpy as np
from jax import lax
from jax.sharding import PartitionSpec as P

DERIV_NEAR = 14.0 / 9.0
DERIV_FAR = 1.0 / 9.0
ALPHA_DERIV = 1.0 / 3.0
ALPHA_FILTER = 0.4999
PRECISE = lax.Precision.HIGHEST


def with_halo(value, sides, width, wrap):
    for axis, dim in sides:
        peers, length = (lax.axis_size(axis), value.shape[dim])
        up = [(i, (i + 1) % peers) for i in range(peers if wrap else peers - 1)]
        down = [(j, i) for i, j in up]
        last = lax.slice_in_dim(value, length - width, length, axis=dim)
        initial = lax.slice_in_dim(value, 0, width, axis=dim)
        before = lax.ppermute(last, axis, up)
        after = lax.ppermute(initial, axis, down)
        value = jnp.concatenate([before, value, after], axis=dim)
    return value


def entering_2(part, axis, combine, identity, reverse):
    count = lax.axis_size(axis)
    place = lax.axis_index(axis)
    ahead = count - 1 - place if reverse else place
    gathered = jax.tree.map(lambda a: lax.all_gather(a, axis), part)
    state = jax.tree.map(lambda a, e: jnp.zeros_like(a) + jnp.asarray(e, a.dtype), part, identity)

    def one(step, state):
        source = count - 1 - step if reverse else step
        return combine(
            state, jax.tree.map(lambda a: lax.dynamic_index_in_dim(a, source, 0, False), gathered)
        )

    return lax.fori_loop(0, ahead, one, state)


def filter_terms(coupling):
    return [
        (193.0 + 126.0 * coupling) / 256.0,
        (105.0 + 302.0 * coupling) / 256.0,
        15.0 * (2.0 * coupling - 1.0) / 64.0,
        45.0 * (1.0 - 2.0 * coupling) / 512.0,
        5.0 * (2.0 * coupling - 1.0) / 256.0,
        (1.0 - 2.0 * coupling) / 512.0,
    ]


def root_of(coupling):
    return (-1.0 + math.sqrt(1.0 - 4.0 * coupling * coupling)) / (2.0 * coupling)


def signed_power(exponent, log_sizes):
    magnitude = jnp.exp(exponent[..., None].astype(jnp.float32) * log_sizes)
    parity = (exponent % 2).astype(jnp.float32)
    return magnitude * (1.0 - 2.0 * parity)[..., None]


def affine_chain(earlier, later):
    return (earlier[0] * later[0], later[0] * earlier[1] + later[1])


def running_products(values):
    result = np.zeros(len(values))
    running = 1.0
    for place in range(len(values)):
        running = running * values[place]
        result[place] = running
    return result


def axial_rhs(shifted, row_index, line_length):
    interior = 0.5 * DERIV_NEAR * (shifted(1) - shifted(-1)) + 0.25 * DERIV_FAR * (
        shifted(2) - shifted(-2)
    )
    row_opening = -2.5 * shifted(0) + 2.0 * shifted(1) + 0.5 * shifted(2)
    row_second = 0.75 * (shifted(1) - shifted(-1))
    row_closing = 2.5 * shifted(0) - 2.0 * shifted(-1) - 0.5 * shifted(-2)
    result = jnp.where(row_index == 0, row_opening, interior)
    result = jnp.where((row_index == 1) | (row_index == line_length - 2), row_second, result)
    return jnp.where(row_index == line_length - 1, row_closing, result)


def bands_table(line_length):
    band_lower = np.full(line_length, ALPHA_DERIV)
    band_lower[0] = 0.0
    band_lower[1] = 0.25
    band_lower[line_length - 2] = 0.25
    band_lower[line_length - 1] = 2.0
    band_middle = np.ones(line_length)
    band_upper = np.full(line_length, ALPHA_DERIV)
    band_upper[0] = 2.0
    band_upper[1] = 0.25
    band_upper[line_length - 2] = 0.25
    band_upper[line_length - 1] = 0.0
    return (band_lower, band_middle, band_upper)


def thomas_tables(line_cells, axial_count):
    line_length = line_cells * axial_count
    band_lower, band_middle, band_upper = bands_table(line_length)
    pivots = np.zeros(line_length)
    factors = np.zeros(line_length)
    pivots[0] = band_middle[0]
    for row_number in range(1, line_length):
        factors[row_number] = -band_lower[row_number] / pivots[row_number - 1]
        pivots[row_number] = (
            band_middle[row_number] + factors[row_number] * band_upper[row_number - 1]
        )
    backs = -band_upper / pivots
    fwd_blocks, fwd_grows, back_blocks, back_grows, inv_pivots = ([], [], [], [], [])
    for place in range(axial_count):
        base_row = place * line_cells
        seg_fwd = factors[base_row : base_row + line_cells]
        seg_back = backs[base_row : base_row + line_cells]
        block_fwd = np.zeros((line_cells, line_cells))
        block_back = np.zeros((line_cells, line_cells))
        for target in range(line_cells):
            running = 1.0
            block_fwd[target, target] = 1.0
            for source in range(target - 1, -1, -1):
                running = running * seg_fwd[source + 1]
                block_fwd[target, source] = running
            running = 1.0
            block_back[target, target] = 1.0
            for source in range(target + 1, line_cells):
                running = running * seg_back[source - 1]
                block_back[target, source] = running
        fwd_blocks.append(block_fwd)
        fwd_grows.append(running_products(seg_fwd))
        back_blocks.append(block_back)
        back_grows.append(running_products(seg_back[::-1])[::-1])
        inv_pivots.append(1.0 / pivots[base_row : base_row + line_cells])
    return [
        jnp.asarray(np.stack(table), jnp.float32)
        for table in (fwd_blocks, fwd_grows, back_blocks, back_grows, inv_pivots)
    ]


def shards(fields):
    cells = fields.shape[2]
    line_cells = fields.shape[3]
    roots = [root_of(ALPHA_DERIV), root_of(ALPHA_FILTER)]
    circ_count = lax.axis_size("circ")
    circ_place = lax.axis_index("circ")
    loop_cells = cells * circ_count
    log_sizes = jnp.asarray([math.log(abs(root_value)) for root_value in roots], jnp.float32)
    wrap_scale = jnp.asarray(
        [1.0 / (1.0 - root_value**loop_cells) for root_value in roots], jnp.float32
    )
    padded = with_halo(fields, (("circ", 2),), 5, True)

    def circ_take(offset):
        return padded[:, :, 5 + offset : 5 + offset + cells, :]

    circ_right = 0.5 * DERIV_NEAR * (circ_take(1) - circ_take(-1)) + 0.25 * DERIV_FAR * (
        circ_take(2) - circ_take(-2)
    )
    terms = filter_terms(ALPHA_FILTER)
    filter_right = terms[0] * circ_take(0)
    for offset in range(1, 6):
        filter_right = filter_right + 0.5 * terms[offset] * (circ_take(offset) + circ_take(-offset))
    scaled = jnp.stack([circ_right * (1.0 + roots[0] ** 2), filter_right * (1.0 + roots[1] ** 2)])
    cell_steps = np.arange(cells)
    cell_gap = cell_steps[:, None] - cell_steps[None, :]
    forward_np = np.stack(
        [
            np.where(cell_gap >= 0, root_value ** np.maximum(cell_gap, 0), 0.0)
            for root_value in roots
        ]
    )
    backward_np = np.stack(
        [
            np.where(cell_gap <= 0, root_value ** np.maximum(-cell_gap, 0), 0.0)
            for root_value in roots
        ]
    )
    forward_table = jnp.asarray(forward_np, jnp.float32)
    backward_table = jnp.asarray(backward_np, jnp.float32)
    grow_forward = jnp.asarray(
        np.stack([root_value ** (cell_steps + 1) for root_value in roots]), jnp.float32
    )
    grow_backward = jnp.asarray(
        np.stack([root_value ** (cells - cell_steps) for root_value in roots]), jnp.float32
    )

    def circ_carry(state, backward):
        piece = lax.all_gather(state[None], "circ", axis=0, tiled=True)
        shard_ids = jnp.arange(piece.shape[0], dtype=jnp.int32)
        if backward:
            distance = (shard_ids - circ_place - 1) % circ_count
        else:
            distance = (circ_place - shard_ids - 1) % circ_count
        weights = signed_power(distance * cells, log_sizes) * wrap_scale
        return jnp.zeros_like(state) + jnp.einsum(
            "qs,qsfna->sfna", weights, piece, precision=PRECISE
        )

    partial_forward = jnp.einsum("sjk,sfnka->sfnja", forward_table, scaled, precision=PRECISE)
    incoming = circ_carry(partial_forward[:, :, :, -1, :], False)
    forward_full = (
        partial_forward + grow_forward[:, None, None, :, None] * incoming[:, :, :, None, :]
    )
    partial_back = jnp.einsum("sjk,sfnka->sfnja", backward_table, forward_full, precision=PRECISE)
    incoming_back = circ_carry(partial_back[:, :, :, 0, :], True)
    solved = partial_back + grow_backward[:, None, None, :, None] * incoming_back[:, :, :, None, :]
    deriv_circ = solved[0]
    filtered = solved[1]
    axial_count = lax.axis_size("ax")
    axial_place = lax.axis_index("ax")
    line_length = line_cells * axial_count
    padded_axial = with_halo(fields, (("ax", 3),), 2, False)

    def axial_take(offset):
        return padded_axial[:, :, :, 2 + offset : 2 + offset + line_cells]

    global_rows = axial_place * line_cells + jnp.arange(line_cells, dtype=jnp.int32)
    axial_right = axial_rhs(axial_take, global_rows, line_length)
    tables = thomas_tables(line_cells, axial_count)
    fwd_block, fwd_grow, back_block, back_grow, inv_pivot = [
        lax.dynamic_index_in_dim(table, axial_place, 0, keepdims=False) for table in tables
    ]

    def axial_carry(multiplier, state, backward):
        identity = (jnp.ones_like(multiplier), jnp.zeros_like(state))
        return entering_2((multiplier, state), "ax", affine_chain, identity, backward)[1]

    local_fwd = jnp.einsum("fnck,jk->fncj", axial_right, fwd_block, precision=PRECISE)
    entering = axial_carry(fwd_grow[-1].reshape(1, 1, 1), local_fwd[:, :, :, -1], False)
    eliminated = (local_fwd + fwd_grow * entering[:, :, :, None]) * inv_pivot
    local_back = jnp.einsum("fnck,jk->fncj", eliminated, back_block, precision=PRECISE)
    entering_back = axial_carry(back_grow[0].reshape(1, 1, 1), local_back[:, :, :, 0], True)
    deriv_axial = local_back + back_grow * entering_back[:, :, :, None]
    return (deriv_circ, deriv_axial, filtered)


def solution(mesh):
    placed = (P(None, None, "circ", "ax"),)
    return jax.shard_map(
        shards,
        mesh=mesh,
        in_specs=placed,
        out_specs=(
            P(None, None, "circ", "ax"),
            P(None, None, "circ", "ax"),
            P(None, None, "circ", "ax"),
        ),
        check_vma=False,
    )
```

profile of v0, /device:TPU:54, one launch (start us, length us, event | category | flops | bytes accessed | tf_op | source)
XLA Modules:
  0.0 285.4 jit_solution(12185485005442516595)
XLA Ops:
  7.2 1.1 fusion.99
  8.3 0.9 collective-permute-start
  9.2 5.7 %collective-permute-start.1 = (f32[3,8,5,256]{3,2,1,0:T(8,128)S(1)}, f32[3,8,5,256]{3,2,1,0:T(8,128)S(1)}, u32[]{:S(2)}, u32[]{:S(2)}) collective-permute-start(f32[3,8,5,256]{3,2,1,0:T(8,128)S(1)} %get-tuple-element.163), channel_id=1, source_target_pairs={{0,4},{4,8},{8,12},{12,16},{16,20},{20,24},{24,28},{28,32},{32,36}... | collective-permute-start | bytes 368648 | tf_op jit(solution)/shard_map/ppermute | solution.py:23
  14.9 0.9 constant_dynamic-update-slice_fusion.1
  15.9 3.7 %collective-permute-done = f32[3,8,5,256]{3,2,1,0:T(8,128)S(1)} collective-permute-done((f32[3,8,5,256]{3,2,1,0:T(8,128)S(1)}, f32[3,8,5,256]{3,2,1,0:T(8,128)S(1)}, u32[]{:S(2)}, u32[]{:S(2)}) %collective-permute-start) | collective-permute-done | bytes 122912 | tf_op jit(solution)/shard_map/ppermute | solution.py:24
  19.6 2.5 multiply_bitcast_fusion
  23.5 123.1 %all-gather.9.cloned.1.call-done = f32[128,3,8,1,256]{4,2,3,1,0:T(8,128)} async-done(((f32[2,3,8,1,256]{4,2,3,1,0:T(8,128)}), f32[128,3,8,1,256]{4,2,3,1,0:T(8,128)}) %all-gather.9.cloned.1.call-update) | async-done | bytes 3145744 | tf_op jit(solution)/shard_map/all_gather | solution.py:195
  146.6 5.1 %fusion.2 = f32[2,1,3,8,256]{4,1,3,2,0:T(1,128)S(1)} fusion(f32[64,2,1,1,1]{0,2,4,3,1:T(1,128)S(1)} %bitcast.83, f32[64,2,3,8,256]{4,3,2,1,0:T(8,128)} %bitcast.77), kind=kOutput, calls=%fused_computation.6 | convolution fusion | flops 9437184 | bytes 3195392 | tf_op jit(solution)/shard_map/qs,qsfna->sfna/dot_general | solution.py:202
  153.1 1.3 collective-permute-start.3
  154.4 3.0 %collective-permute-start.2 = (f32[3,8,8,2]{3,2,1,0:T(8,128)S(1)}, f32[3,8,8,2]{3,2,1,0:T(8,128)S(1)}, u32[]{:S(2)}, u32[]{:S(2)}) collective-permute-start(f32[3,8,8,2]{3,2,1,0:T(8,128)S(1)} %get-tuple-element.159), channel_id=1, source_target_pairs={{0,1},{1,2},{2,3},{4,5},{5,6},{6,7},{8,9},{9,10},{10,11},{12,13},{... | collective-permute-start | bytes 4616 | tf_op jit(solution)/shard_map/ppermute | solution.py:23
  158.0 1.3 dynamic-slice.2
  159.3 1.3 bitcast_dynamic-update-slice_fusion.1
  160.6 1.4 bitcast_dynamic-update-slice_fusion
  162.8 0.7 constant_dynamic-slice_fusion.3
  163.5 7.8 %all-reduce.2 = (f32[4]{0:T(128)S(1)}, f32[4]{0:T(128)S(1)}) all-reduce(f32[4]{0:T(128)S(1)} %bitcast_dynamic-update-slice_fusion.1, f32[4]{0:T(128)S(1)} %bitcast_dynamic-update-slice_fusion), channel_id=4, replica_groups=mesh['circ'=64,'ax'=4] {'ax'}, use_global_device_ids=true, to_apply=%add | all-reduce | flops 8 | bytes 64
  171.3 1.5 fusion.11
  173.1 5.2 %all-gather.3 = f32[12,8,8,1]{2,1,3,0:T(8,128)S(1)} all-gather(f32[3,8,8,1]{2,1,3,0:T(8,128)S(1)} %copy.21), channel_id=5, replica_groups=mesh['circ'=64,'ax'=4] {'ax'}, dimensions={0}, use_global_device_ids=true | all-gather | bytes 3840 | tf_op jit(solution)/shard_map/all_gather | solution.py:33
  178.3 1.4 fusion.9
  179.9 8.5 %all-gather.5 = f32[12,8,8,1]{2,1,3,0:T(8,128)S(1)} all-gather(f32[3,8,8,1]{2,1,3,0:T(8,128)S(1)} %copy.22), channel_id=7, replica_groups=mesh['circ'=64,'ax'=4] {'ax'}, dimensions={0}, use_global_device_ids=true | all-gather | bytes 3840 | tf_op jit(solution)/shard_map/all_gather | solution.py:33
  188.4 4.0 %while.27 = (s32[]{:T(128)}, f32[3,8,8]{2,1,0:T(8,128)S(1)}, s32[]{:T(128)}, f32[4,1,1,1]{0,3,2,1:T(1,128)S(1)}, f32[4,3,8,8]{3,2,1,0:T(8,128)S(1)}, /*index=5*/s32[]{:T(128)}, s32[]{:T(128)}, s32[]{:T(128)}, s32[]{:T(128)}) while((s32[]{:T(128)}, f32[3,8,8]{2,1,0:T(8,128)S(1)}, s32[]{:T(128)}, f32[4,1,1,1]{0,3,2,1:T(1,128)S(1)}, ...), condition=%wide.region_3.4_spmd, body=%wide.region_2.3_spmd.sunk | while | flops 390 | bytes 2463 | solution.py:42
  192.4 0.8 multiply_add_fusion.1
  193.2 79.4 %all-gather.11.cloned.1.call-done = f32[128,3,8,1,256]{4,2,3,1,0:T(8,128)} async-done(((f32[2,3,8,1,256]{4,2,3,1,0:T(8,128)}), f32[128,3,8,1,256]{4,2,3,1,0:T(8,128)}) %all-gather.11.cloned.1.call-update) | async-done | bytes 3145744 | tf_op jit(solution)/shard_map/all_gather | solution.py:195
  272.6 5.1 %fusion = f32[2,1,3,8,256]{4,1,3,2,0:T(1,128)S(1)} fusion(f32[64,2,1,1,1]{0,2,4,3,1:T(1,128)S(1)} %bitcast.82, f32[64,2,3,8,256]{4,3,2,1,0:T(8,128)} %bitcast.76), kind=kOutput, calls=%fused_computation.4 | convolution fusion | flops 9437184 | bytes 3195392 | tf_op jit(solution)/shard_map/qs,qsfna->sfna/dot_general | solution.py:202
  277.8 0.8 slice_bitcast_fusion
  (57 shorter events, 8.3 us)
Async XLA Ops:
  7.2 15.0 %copy-start.2 = (f32[2,8,8,1,1]{2,1,4,3,0:T(8,128)S(1)}, f32[2,8,8,1,1]{2,1,4,3,0:T(8,128)}, u32[]{:S(2)}) copy-start(f32[2,8,8,1,1]{2,1,4,3,0:T(8,128)} %constant.206) | copy-start | bytes 1540
  7.2 16.3 %copy-start.5 = (f32[2]{0:T(128)S(1)}, f32[2]{0:T(128)}, u32[]{:S(2)}) copy-start(f32[2]{0:T(128)} %constant.182.clone) | copy-start | bytes 28
  7.2 16.3 %copy-start.6 = (f32[2]{0:T(128)S(1)}, f32[2]{0:T(128)}, u32[]{:S(2)}) copy-start(f32[2]{0:T(128)} %constant.183.clone) | copy-start | bytes 28
  7.2 139.4 %all-gather.9.cloned.1.call-start = ((), (), s32[]{:S(2)}) async-start(), calls=%async_computation | async-start | bytes 3194880 | tf_op jit(solution)/shard_map/all_gather | solution.py:195
  8.3 11.2 %collective-permute-start = (f32[3,8,5,256]{3,2,1,0:T(8,128)S(1)}, f32[3,8,5,256]{3,2,1,0:T(8,128)S(1)}, u32[]{:S(2)}, u32[]{:S(2)}) collective-permute-start(f32[3,8,5,256]{3,2,1,0:T(8,128)S(1)} %get-tuple-element.162), channel_id=1, source_target_pairs={{4,0},{8,4},{12,8},{16,12},{20,16},{24,20},{28,24},{32,28},{36,32}... | collective-permute-start | bytes 368648 | tf_op jit(solution)/shard_map/ppermute | solution.py:24
  9.2 10.4 %collective-permute-start.1 = (f32[3,8,5,256]{3,2,1,0:T(8,128)S(1)}, f32[3,8,5,256]{3,2,1,0:T(8,128)S(1)}, u32[]{:S(2)}, u32[]{:S(2)}) collective-permute-start(f32[3,8,5,256]{3,2,1,0:T(8,128)S(1)} %get-tuple-element.163), channel_id=1, source_target_pairs={{0,4},{4,8},{8,12},{12,16},{16,20},{20,24},{24,28},{28,32},{32,36}... | collective-permute-start | bytes 368648 | tf_op jit(solution)/shard_map/ppermute | solution.py:23
  19.6 132.2 %copy-start.1 = (f32[2,8,8,1,1]{2,1,4,3,0:T(8,128)S(1)}, f32[2,8,8,1,1]{2,1,4,3,0:T(8,128)}, u32[]{:S(2)}) copy-start(f32[2,8,8,1,1]{2,1,4,3,0:T(8,128)} %constant.207) | copy-start | bytes 1540
  19.6 132.2 %copy-start.4 = (f32[2,8]{1,0:T(2,128)S(1)}, f32[2,8]{1,0:T(2,128)}, u32[]{:S(2)}) copy-start(f32[2,8]{1,0:T(2,128)} %constant.186.clone) | copy-start | bytes 196
  22.1 130.9 %copy-start = (f32[3,8,8,256]{3,2,1,0:T(8,128)S(1)}, f32[3,8,8,256]{3,2,1,0:T(8,128)}, u32[]{:S(2)}) copy-start(f32[3,8,8,256]{3,2,1,0:T(8,128)} %param.16) | copy-start | bytes 589828
  22.1 135.3 %copy-start.7 = (u32[256]{0:T(256)S(1)}, u32[256]{0:T(256)}, u32[]{:S(2)}) copy-start(u32[256]{0:T(256)} %constant.196) | copy-start | bytes 3076
  23.3 249.3 %all-gather.11.cloned.1.call-start = ((), (), s32[]{:S(2)}) async-start(), calls=%async_computation.1 | async-start | bytes 3194880 | tf_op jit(solution)/shard_map/all_gather | solution.py:195
  153.1 18.2 %collective-permute-start.3 = (f32[3,8,8,2]{3,2,1,0:T(8,128)S(1)}, f32[3,8,8,2]{3,2,1,0:T(8,128)S(1)}, u32[]{:S(2)}, u32[]{:S(2)}) collective-permute-start(f32[3,8,8,2]{3,2,1,0:T(8,128)S(1)} %get-tuple-element.160), channel_id=1, source_target_pairs={{1,0},{2,1},{3,2},{5,4},{6,5},{7,6},{9,8},{10,9},{11,10},{13,12},{... | collective-permute-start | bytes 4616 | tf_op jit(solution)/shard_map/ppermute | solution.py:24
  154.4 16.9 %collective-permute-start.2 = (f32[3,8,8,2]{3,2,1,0:T(8,128)S(1)}, f32[3,8,8,2]{3,2,1,0:T(8,128)S(1)}, u32[]{:S(2)}, u32[]{:S(2)}) collective-permute-start(f32[3,8,8,2]{3,2,1,0:T(8,128)S(1)} %get-tuple-element.159), channel_id=1, source_target_pairs={{0,1},{1,2},{2,3},{4,5},{5,6},{6,7},{8,9},{9,10},{10,11},{12,13},{... | collective-permute-start | bytes 4616 | tf_op jit(solution)/shard_map/ppermute | solution.py:23
  172.8 104.9 %copy-start.3 = (f32[2,8]{1,0:T(2,128)S(1)}, f32[2,8]{1,0:T(2,128)}, u32[]{:S(2)}) copy-start(f32[2,8]{1,0:T(2,128)} %constant.187.clone) | copy-start | bytes 196
Sparse Core Ops, SparseCore 0:
  23.4 123.1 all-gather.8
  153.1 119.4 all-gather.10
where the time goes:
time: 289 us; the launch traced here: 285 us
  waiting for transfers between devices  206 us (71%)
  blocking collectives  21.5 us (7%)
  between operations  14.4 us (5%)
  matrix products  14.1 us (5%)
  local copies, waits for them, and re-layouts  12.5 us (4%)
  starting transfers between devices  11 us (4%)
  other arithmetic  5.51 us (2%)
    all_gather x2, waiting for transfers between devices, circ_carry(): piece = lax.all_gather(state[None], 'circ', axis=0, tiled=True)  203 us
    all_gather x2, blocking collectives, entering_2(): gathered = jax.tree.map(lambda a: lax.all_gather(a, axis), part)  13.7 us
    dot_general x2, matrix products, circ_carry(): jnp.einsum('qs,qsfna->sfna', weights, piece, precision=PRECISE)  10.2 us
    ppermute x2, starting transfers between devices, with_halo(): before = lax.ppermute(last, axis, up)  8.75 us
    unnamed x1, blocking collectives  7.77 us
  transfers between devices with their start and end apart: 6, of which 3 were waited for; matrix products, arithmetic and copies ran while one was open for 5% of the time, Pallas kernels for 0%

commit v1 on v0

v1 whole, which is shorter than its diff:
```python
import functools
import math

import jax
import jax.numpy as jnp
import numpy as np
from jax import lax
from jax.experimental import pallas as pl
from jax.experimental.pallas import tpu as pltpu
from jax.sharding import PartitionSpec as P

DERIV_NEAR = 14.0 / 9.0
DERIV_FAR = 1.0 / 9.0
ALPHA_DERIV = 1.0 / 3.0
ALPHA_FILTER = 0.4999
PRECISE = lax.Precision.HIGHEST
REACH = 4


def filter_terms(coupling):
    return [
        (193.0 + 126.0 * coupling) / 256.0,
        (105.0 + 302.0 * coupling) / 256.0,
        15.0 * (2.0 * coupling - 1.0) / 64.0,
        45.0 * (1.0 - 2.0 * coupling) / 512.0,
        5.0 * (2.0 * coupling - 1.0) / 256.0,
        (1.0 - 2.0 * coupling) / 512.0,
    ]


def root_of(coupling):
    return (-1.0 + math.sqrt(1.0 - 4.0 * coupling * coupling)) / (2.0 * coupling)


def stencils():
    deriv = {
        1: 0.5 * DERIV_NEAR,
        -1: -0.5 * DERIV_NEAR,
        2: 0.25 * DERIV_FAR,
        -2: -0.25 * DERIV_FAR,
    }
    terms = filter_terms(ALPHA_FILTER)
    smooth = {0: terms[0]}
    for offset in range(1, 6):
        smooth[offset] = smooth[-offset] = 0.5 * terms[offset]
    return [(ALPHA_DERIV, deriv), (ALPHA_FILTER, smooth)]


def line_kernel(coupling, stencil):
    root = root_of(coupling)
    gain = 1.0 / (1.0 + 2.0 * coupling * root)

    def h(n):
        return gain * math.fsum(c * root ** abs(n + m) for m, c in stencil.items())

    right = gain * math.fsum(c * root**m for m, c in stencil.items())
    left = gain * math.fsum(c * root ** (-m) for m, c in stencil.items())
    return root, h, right, left


def circ_tables(cells):
    local = np.zeros((2, cells, cells))
    halo = np.zeros((2, cells, cells))
    for which, (coupling, stencil) in enumerate(stencils()):
        root, h, right, left = line_kernel(coupling, stencil)
        for i in range(cells):
            for k in range(cells):
                local[which, i, k] = h(i - k)
            for m in range(cells):
                n = i - (cells + m) if m < REACH else i - (m - cells)
                if 0 < abs(n) <= REACH:
                    halo[which, i, m] = h(n) - (right if n > 0 else left) * root ** abs(n)
    return local, halo


def carry_tables(cells, count):
    rounds = count.bit_length() - 1
    table = np.zeros((count, rounds + 1, 4))
    merge = np.zeros((rounds, 2))
    for which, (coupling, stencil) in enumerate(stencils()):
        root, _, right, left = line_kernel(coupling, stencil)
        step = root**cells
        wrap = 1.0 / (1.0 - step**count)
        for k in range(rounds):
            merge[k, which] = step ** (1 << k)
        for p in range(count):
            for k in range(rounds):
                size = 1 << k
                start = (p >> k) << k
                end = start + size - 1
                last = k == rounds - 1
                factor = wrap if last else 1.0
                if (p >> k) & 1:
                    table[p, k, 2 * which] = right * factor * step ** (p - start)
                    if last:
                        table[p, k, 2 * which + 1] = left * factor * step ** (count - 1 - p)
                else:
                    table[p, k, 2 * which + 1] = left * factor * step ** (end - p)
                    if last:
                        table[p, k, 2 * which] = right * factor * step**p
                if last:
                    table[p, rounds, 2 * which] = right * wrap * step ** (p + count - 1 - end)
                    table[p, rounds, 2 * which + 1] = left * wrap * step ** (start + count - 1 - p)
    return table, merge


def bands_table(line_length):
    band_lower = np.full(line_length, ALPHA_DERIV)
    band_lower[0] = 0.0
    band_lower[1] = 0.25
    band_lower[line_length - 2] = 0.25
    band_lower[line_length - 1] = 2.0
    band_upper = np.full(line_length, ALPHA_DERIV)
    band_upper[0] = 2.0
    band_upper[1] = 0.25
    band_upper[line_length - 2] = 0.25
    band_upper[line_length - 1] = 0.0
    return band_lower, band_upper


def axial_stencil(line_length):
    s = np.zeros((line_length, line_length))
    for k in range(2, line_length - 2):
        s[k, k + 1] = 0.5 * DERIV_NEAR
        s[k, k - 1] = -0.5 * DERIV_NEAR
        s[k, k + 2] = 0.25 * DERIV_FAR
        s[k, k - 2] = -0.25 * DERIV_FAR
    s[0, :3] = (-2.5, 2.0, 0.5)
    s[1, 0], s[1, 2] = -0.75, 0.75
    e = line_length - 1
    s[e - 1, e - 2], s[e - 1, e] = -0.75, 0.75
    s[e, e - 2 : e + 1] = (-0.5, -2.0, 2.5)
    return s


def axial_tables(line_cells, count):
    n = line_cells * count
    low, up = bands_table(n)
    s = axial_stencil(n)
    t = np.eye(n) + np.diag(low[1:], -1) + np.diag(up[:-1], 1)
    inverse = np.linalg.inv(t)
    full = inverse @ s
    from_top = np.zeros(n)
    from_top[0] = 1.0
    for i in range(1, n):
        from_top[i] = 1.0 - low[i] * up[i - 1] / from_top[i - 1]
    from_end = np.zeros(n)
    from_end[n - 1] = 1.0
    for i in range(n - 2, -1, -1):
        from_end[i] = 1.0 - up[i] * low[i + 1] / from_end[i + 1]
    down = -low / from_end
    back = -up / from_top
    local = np.zeros((count, line_cells, line_cells))
    gather = np.zeros((count, 4, line_cells))
    grow_down = np.zeros((count, line_cells))
    grow_back = np.zeros((count, line_cells))
    corner = np.zeros((count, 2))
    for p in range(count):
        b, e = p * line_cells, (p + 1) * line_cells
        local[p] = full[b:e, b:e]
        grow_down[p] = np.cumprod(down[b:e])
        grow_back[p] = np.cumprod(back[b:e][::-1])[::-1]
        gather[p, 2, 0] = 1.0
        gather[p, 3, line_cells - 1] = 1.0
        if e < n:
            y = inverse[e - 1].copy()
            y[e:] = 0.0
            for k in range(e, e + 2):
                y[k] = inverse[k, k] / np.prod(down[e : k + 1])
            gather[p, 0] = (y @ s)[b:e]
        if b > 0:
            y = inverse[b].copy()
            y[:b] = 0.0
            for k in range(b - 2, b):
                y[k] = inverse[k, k] / np.prod(back[k:b])
            gather[p, 1] = (y @ s)[b:e]
    for p in range(count):
        b, e = p * line_cells, (p + 1) * line_cells
        if p > 0:
            corner[p, 0] = full[b, b - 1] - grow_down[p, 0] * gather[p - 1, 0, -1]
        if p < count - 1:
            corner[p, 1] = full[e - 1, e] - grow_back[p, -1] * gather[p + 1, 1, 0]
    spread = np.zeros((count, count, 4, line_cells))
    for p in range(count):
        weight = 1.0
        for q in range(p - 1, -1, -1):
            spread[p, q, 0] = weight * grow_down[p]
            weight *= grow_down[q, -1]
        weight = 1.0
        for q in range(p + 1, count):
            spread[p, q, 1] = weight * grow_back[p]
            weight *= grow_back[q, 0]
        if p > 0:
            spread[p, p - 1, 3, 0] = corner[p, 0]
        if p < count - 1:
            spread[p, p + 1, 2, -1] = corner[p, 1]
    return local, gather, spread


def by_row(values, shape):
    rows = lax.broadcasted_iota(jnp.int32, shape, len(shape) - 2)
    out = jnp.full(shape, float(values[0]), jnp.float32)
    for i in range(1, len(values)):
        out = jnp.where(rows == i, jnp.float32(values[i]), out)
    return out


def totals_kernel(weights, u_ref, s_ref, first_ref, last_ref):
    lines, cells, width = u_ref.shape
    w = [by_row(weights[v], (cells, width)) for v in range(4)]
    for n in range(lines):
        un = u_ref[n]
        for v in range(4):
            s_ref[v, n : n + 1, :] = jnp.sum(un * w[v], axis=0, keepdims=True)
        first_ref[n] = un[:REACH]
        last_ref[n] = un[cells - REACH :]


def near_kernel(local, halo, u_ref, right_ref, left_ref, d_ref, f_ref):
    lines, cells, width = u_ref.shape
    outs = (d_ref, f_ref)
    diag = {}
    for name, table in (("local", local), ("halo", halo)):
        for which in range(2):
            for s in range(cells):
                values = [table[which, i, (i - s) % cells] for i in range(cells)]
                if np.any(np.asarray(values) != 0.0):
                    diag[name, which, s] = by_row(values, (cells, width))
    for n in range(lines):
        un = u_ref[n]
        hn = jnp.concatenate([right_ref[n], left_ref[n]], axis=0)
        acc = [None, None]
        for name, value in (("local", un), ("halo", hn)):
            for s in range(cells):
                used = [w for w in range(2) if (name, w, s) in diag]
                if not used:
                    continue
                turned = pltpu.roll(value, s, 0) if s else value
                for w in used:
                    term = turned * diag[name, w, s]
                    acc[w] = term if acc[w] is None else acc[w] + term
        for w in range(2):
            outs[w][n] = acc[w]


def far_kernel(rounds, roots, coef_ref, *refs):
    got = refs[: rounds + 1]
    d_near, f_near, d_ref, f_ref, lr = refs[rounds + 1 :]
    lines, cells, width = d_near.shape
    for v in range(4):
        total = got[0][v] * coef_ref[0, v]
        for k in range(1, rounds + 1):
            total = total + got[k][v] * coef_ref[k, v]
        lr[v] = total
    near = (d_near, f_near)
    outs = (d_ref, f_ref)
    for which in range(2):
        a = by_row([roots[which] ** (i + 1) for i in range(cells)], (cells, width))
        b = by_row([roots[which] ** (cells - i) for i in range(cells)], (cells, width))
        for n in range(lines):
            from_left = jnp.broadcast_to(lr[2 * which, n : n + 1, :], (cells, width))
            from_right = jnp.broadcast_to(lr[2 * which + 1, n : n + 1, :], (cells, width))
            outs[which][n] = near[which][n] + a * from_left + b * from_right


def vmem(count):
    return [pl.BlockSpec(memory_space=pltpu.VMEM)] * count


def shards(fields):
    parts, radial, cells, width = fields.shape
    lines = parts * radial
    u = fields.reshape(lines, cells, width)
    circ_count = lax.axis_size("circ")
    circ_place = lax.axis_index("circ")
    ax_count = lax.axis_size("ax")
    ax_place = lax.axis_index("ax")
    rounds = circ_count.bit_length() - 1
    roots = [root_of(ALPHA_DERIV), root_of(ALPHA_FILTER)]
    f32 = jnp.float32

    weights = np.zeros((4, cells))
    for which, root in enumerate(roots):
        weights[2 * which] = root ** (cells - 1.0 - np.arange(cells))
        weights[2 * which + 1] = root ** (1.0 * np.arange(cells))
    totals, first, last = pl.pallas_call(
        functools.partial(totals_kernel, weights),
        out_shape=(
            jax.ShapeDtypeStruct((4, lines, width), f32),
            jax.ShapeDtypeStruct((lines, REACH, width), f32),
            jax.ShapeDtypeStruct((lines, REACH, width), f32),
        ),
        in_specs=vmem(1),
        out_specs=tuple(vmem(3)),
        name="totals",
    )(u)

    table, merge = carry_tables(cells, circ_count)
    coef = lax.dynamic_index_in_dim(jnp.asarray(table, f32), circ_place, 0, False)
    masks = [1, 3, 4, 8, 16, 48]
    got = []
    for k in range(rounds):
        other = lax.ppermute(totals, "circ", [(i, i ^ masks[k]) for i in range(circ_count)])
        got.append(other)
        if k < rounds - 1:
            on_right = ((circ_place >> k) & 1) == 1
            grow = [float(merge[k, 0]), float(merge[k, 1])]
            own, their = [], []
            for which in range(2):
                one = jnp.float32(1.0)
                g = jnp.float32(grow[which])
                own += [jnp.where(on_right, one, g), jnp.where(on_right, g, one)]
                their += [jnp.where(on_right, g, one), jnp.where(on_right, one, g)]
            totals = jnp.stack([own[v] * totals[v] + their[v] * other[v] for v in range(4)])
    got.append(totals)

    ring = [(i, (i + 1) % circ_count) for i in range(circ_count)]
    gnir = [(j, i) for i, j in ring]
    left = lax.ppermute(last, "circ", ring)
    right = lax.ppermute(first, "circ", gnir)

    local, halo = circ_tables(cells)
    d_near, f_near = pl.pallas_call(
        functools.partial(near_kernel, local, halo),
        out_shape=(jax.ShapeDtypeStruct(u.shape, f32),) * 2,
        in_specs=vmem(3),
        out_specs=tuple(vmem(2)),
        name="near",
    )(u, right, left)

    ax_local, ax_gather, ax_spread = axial_tables(width, ax_count)
    rows = u.reshape(lines * cells, width)
    mine = lax.dynamic_index_in_dim(jnp.asarray(ax_gather, f32), ax_place, 0, False)
    sent = lax.dot_general(mine, rows, (((1,), (1,)), ((), ())), precision=PRECISE)
    near_side = lax.ppermute(sent, "ax", [(i, i ^ 1) for i in range(ax_count)])
    pair = jnp.concatenate([sent, near_side], axis=0)
    far_side = lax.ppermute(pair, "ax", [(i, i ^ 2) for i in range(ax_count)])
    order = np.asarray([[p ^ 1, p ^ 2, p ^ 3] for p in range(ax_count)])
    spread = np.stack([ax_spread[p][order[p]].reshape(12, width) for p in range(ax_count)])
    spread = lax.dynamic_index_in_dim(jnp.asarray(spread, f32), ax_place, 0, False)
    square = lax.dynamic_index_in_dim(jnp.asarray(ax_local.swapaxes(1, 2), f32), ax_place, 0, False)
    ax_in = jnp.concatenate([near_side, far_side], axis=0)
    ax_out = jnp.dot(rows, square, precision=PRECISE)
    ax_out = ax_out + lax.dot_general(ax_in, spread, (((0,), (0,)), ((), ())), precision=PRECISE)

    d_circ, filtered = pl.pallas_call(
        functools.partial(far_kernel, rounds, roots),
        out_shape=(jax.ShapeDtypeStruct(u.shape, f32),) * 2,
        in_specs=[pl.BlockSpec(memory_space=pltpu.SMEM)] + vmem(rounds + 3),
        out_specs=tuple(vmem(2)),
        scratch_shapes=[pltpu.VMEM((4, lines, width), f32)],
        name="far",
    )(coef, *got, d_near, f_near)
    shape = fields.shape
    return d_circ.reshape(shape), ax_out.reshape(shape), filtered.reshape(shape)


def solution(mesh):
    spec = P(None, None, "circ", "ax")
    return jax.shard_map(
        shards, mesh=mesh, in_specs=(spec,), out_specs=(spec, spec, spec), check_vma=False
    )
```

time: 289 us -> 52.1 us (0.18); the launches traced: 285 us -> 51.7 us
  waiting for transfers between devices: 206 us -> 14.5 us
  blocking collectives: 21.5 us -> 0 us
  between operations: 14.4 us -> 0.78 us
  matrix products: 14.1 us -> 3.95 us
  starting transfers between devices: 11 us -> 19.5 us
  local copies, waits for them, and re-layouts: 12.5 us -> 5.8 us
  Pallas kernels: 0 us -> 6.2 us
  other arithmetic: 5.51 us -> 0.98 us
    all_gather x2 -> x0, waiting for transfers between devices: 203 us -> none  [circ_carry(): piece = lax.all_gather(state[None], 'circ', axis=0, tiled=True)]
    all_gather x2 -> x0, blocking collectives: 13.7 us -> none  [entering_2(): gathered = jax.tree.map(lambda a: lax.all_gather(a, axis), part)]
    ppermute x4 -> x10, waiting for transfers between devices: 3.68 us -> 14.5 us  [the longest x6 14.5 us: shards(): lax.ppermute(totals, 'circ', [(i, i ^ masks[k]) for i in range(circ_count)])]
    dot_general x6 -> x3, matrix products: 14.1 us -> 3.95 us  [the longest x1 1.76 us: shards(): lax.dot_general(ax_in, spread, (((0,), (0,)), ((), ())), precision=PRECISE)]
    ppermute x4 -> x10, starting transfers between devices: 10.9 us -> 19.5 us  [the longest x6 11.5 us: shards(): lax.ppermute(totals, 'circ', [(i, i ^ masks[k]) for i in range(circ_count)])]
    unnamed x1 -> x0, blocking collectives: 7.77 us -> none
    pallas_call x0 -> x3, Pallas kernels: none -> 6.2 us  [the longest x1 2.24 us: shards(): pl.pallas_call(functools.partial(near_kernel, local, halo), out_shape=(ja...]
    slice x11 -> x0, local copies, waits for them, and re-layouts: 4.24 us -> none  [the longest x1 1.28 us: shards(): fwd_grow[-1].reshape(1, 1, 1)]
  transfers between devices with their start and end apart: 6 -> 10, of which waited for: 3 -> 4; matrix products, arithmetic and copies ran while one was open for 5% -> 12% of each run, Pallas kernels for 0% -> 4%
where the time goes in v1:
time: 52.1 us; the launch traced here: 51.7 us
  starting transfers between devices  19.5 us (37%)
  waiting for transfers between devices  14.5 us (28%)
  Pallas kernels  6.2 us (12%)
  local copies, waits for them, and re-layouts  5.8 us (11%)
  matrix products  3.95 us (8%)
  other arithmetic  0.98 us (2%)
  between operations  0.78 us (1%)
    ppermute x6, waiting for transfers between devices, shards(): lax.ppermute(totals, 'circ', [(i, i ^ masks[k]) for i in range(circ_count)])  14.5 us
    ppermute x6, starting transfers between devices, shards(): lax.ppermute(totals, 'circ', [(i, i ^ masks[k]) for i in range(circ_count)])  11.5 us
    ppermute x1, starting transfers between devices, shards(): left = lax.ppermute(last, 'circ', ring)  5.34 us
    unnamed x20, local copies, waits for them, and re-layouts  4.43 us
    pallas_call x1, Pallas kernels, shards(): pl.pallas_call(functools.partial(near_kernel, local, halo), out_shape=(ja...  2.24 us
    pallas_call x1, Pallas kernels, shards(): pl.pallas_call(functools.partial(far_kernel, rounds, roots), out_shape=(j...  2.14 us
    pallas_call x1, Pallas kernels, shards(): pl.pallas_call(functools.partial(totals_kernel, weights), out_shape=(jax....  1.83 us
    dot_general x1, matrix products, shards(): lax.dot_general(ax_in, spread, (((0,), (0,)), ((), ())), precision=PRECISE)  1.76 us
  transfers between devices with their start and end apart: 10, of which 4 were waited for; matrix products, arithmetic and copies ran while one was open for 12% of the time, Pallas kernels for 4%

profile of v1, /device:TPU:54, one launch (start us, length us, event | category | flops | bytes accessed | tf_op | source)
XLA Modules:
  0.0 51.7 jit_solution(3438216110923714731)
XLA Ops:
  0.6 1.8 %totals.1 = (f32[4,24,256]{2,1,0:T(8,128)}, f32[24,4,256]{2,1,0:T(4,128)}, f32[24,4,256]{2,1,0:T(4,128)}) custom-call(f32[24,8,256]{2,1,0:T(8,128)} %bitcast.20), custom_call_target="tpu_custom_call" | custom-call | tf_op jit(solution)/shard_map/totals/pallas_call | solution.py:286
  2.5 0.8 %collective-permute-start = (f32[4,24,256]{2,1,0:T(8,128)}, f32[4,24,256]{2,1,0:T(8,128)S(1)}, u32[]{:S(2)}, u32[]{:S(2)}) collective-permute-start(f32[4,24,256]{2,1,0:T(8,128)} %get-tuple-element.10), channel_id=1, source_target_pairs={{0,4},{4,0},{8,12},{12,8},{16,20},{20,16},{24,28},{28,24},{32,36},... | collective-permute-start | bytes 294920 | tf_op jit(solution)/shard_map/ppermute | solution.py:303
  3.3 1.2 %collective-permute-start.6 = (f32[24,4,256]{2,1,0:T(4,128)}, f32[24,4,256]{2,1,0:T(4,128)S(1)}, u32[]{:S(2)}, u32[]{:S(2)}) collective-permute-start(f32[24,4,256]{2,1,0:T(4,128)} %get-tuple-element.11), channel_id=1, source_target_pairs={{4,0},{8,4},{12,8},{16,12},{20,16},{24,20},{28,24},{32,28},{36,32}... | collective-permute-start | bytes 294920 | tf_op jit(solution)/shard_map/ppermute | solution.py:320
  4.5 5.3 %collective-permute-start.7 = (f32[24,4,256]{2,1,0:T(4,128)}, f32[24,4,256]{2,1,0:T(4,128)S(1)}, u32[]{:S(2)}, u32[]{:S(2)}) collective-permute-start(f32[24,4,256]{2,1,0:T(4,128)} %get-tuple-element.12), channel_id=1, source_target_pairs={{0,4},{4,8},{8,12},{12,16},{16,20},{20,24},{24,28},{28,32},{32,36}... | collective-permute-start | bytes 294920 | tf_op jit(solution)/shard_map/ppermute | solution.py:319
  9.8 0.9 %fusion.21 = (f32[1,24,256]{2,1,0:T(8,128)S(1)}, f32[1,24,256]{2,1,0:T(8,128)S(1)}, f32[1,24,256]{2,1,0:T(8,128)S(1)}, f32[1,24,256]{2,1,0:T(8,128)S(1)}) fusion(f32[4,24,256]{2,1,0:T(8,128)S(1)} %collective-permute-done.refs_0_, f32[4,24,256]{2,1,0:T(8,128)} %get-tuple-element.10, f32[]{:T(128)S(6)} %select_n.95, f32[]{:T(128)S(6)} %select_n.94, ...), kind=kLoop, calls=%fused_computation.48 | loop fusion | flops 73728 | bytes 294928 | tf_op jit(solution)/shard_map/add | solution.py:314
  10.9 0.9 %fusion.27 = f32[4,192]{1,0:T(4,128)S(1)} fusion(f32[192,256]{1,0:T(8,128)S(1)} %bitcast.22, f32[4,4,256]{2,1,0:T(4,128)} %constant.67.clone, s32[]{:T(128)S(6)} %select_n.114), kind=kOutput, calls=%fused_computation.55 | convolution fusion | flops 2359296 | bytes 203780 | tf_op jit(solution)/shard_map/dot_general | solution.py:334
  11.8 4.8 %collective-permute-done.1.refs_1_ = f32[4,24,256]{2,1,0:T(8,128)S(1)} collective-permute-done((f32[4,24,256]{2,1,0:T(8,128)S(1)}, f32[4,24,256]{2,1,0:T(8,128)S(1)}, u32[]{:S(2)}, u32[]{:S(2)}) %collective-permute-start.1) | collective-permute-done | bytes 98336 | tf_op jit(solution)/shard_map/ppermute | solution.py:303
  16.7 0.6 %copy-done.2 = f32[4,24,256]{2,1,0:T(8,128)} copy-done((f32[4,24,256]{2,1,0:T(8,128)}, f32[4,24,256]{2,1,0:T(8,128)S(1)}, u32[]{:S(2)}) %copy-start.2) | copy-done | bytes 98328
  17.4 1.3 %convolution_bitcast_fusion = f32[192,256]{1,0:T(8,128)S(1)} fusion(f32[192,256]{1,0:T(8,128)S(1)} %bitcast.23, f32[4,256,256]{2,1,0:T(8,128)} %constant.69.clone, s32[]{:T(128)S(6)} %select_n.114), kind=kOutput, calls=%fused_computation | convolution fusion | flops 150994944 | bytes 655364 | tf_op jit(solution)/shard_map/dot_general | solution.py:343
  18.7 4.8 %collective-permute-done.2.refs_2_ = f32[4,24,256]{2,1,0:T(8,128)S(1)} collective-permute-done((f32[4,24,256]{2,1,0:T(8,128)S(1)}, f32[4,24,256]{2,1,0:T(8,128)S(1)}, u32[]{:S(2)}, u32[]{:S(2)}) %collective-permute-start.2) | collective-permute-done | bytes 98336 | tf_op jit(solution)/shard_map/ppermute | solution.py:303
  23.5 0.6 %copy-done.3 = f32[4,24,256]{2,1,0:T(8,128)} copy-done((f32[4,24,256]{2,1,0:T(8,128)}, f32[4,24,256]{2,1,0:T(8,128)S(1)}, u32[]{:S(2)}) %copy-start.3) | copy-done | bytes 98328
  24.3 0.7 %dynamic-slice_bitcast_fusion = f32[7,4]{0,1:T(4,128)S(1)} fusion(f32[64,7,4]{1,2,0:T(4,128)} %constant.66.clone, s32[]{:T(128)S(6)} %select_n.93), kind=kLoop, calls=%fused_computation.58 | loop fusion | bytes 228 | tf_op jit(solution)/shard_map/jit(dynamic_index_in_dim)/squeeze | solution.py:299
  25.0 0.7 %copy.8.coef_ref = f32[7,4]{1,0:T(8,128)} copy(f32[7,4]{0,1:T(4,128)S(1)} %dynamic-slice_bitcast_fusion) | data formatting | bytes 224 | tf_op jit(solution)/shard_map/jit(dynamic_index_in_dim)/squeeze | solution.py:299
  25.7 3.1 %collective-permute-done.3.refs_3_ = f32[4,24,256]{2,1,0:T(8,128)S(1)} collective-permute-done((f32[4,24,256]{2,1,0:T(8,128)S(1)}, f32[4,24,256]{2,1,0:T(8,128)S(1)}, u32[]{:S(2)}, u32[]{:S(2)}) %collective-permute-start.3) | collective-permute-done | bytes 98336 | tf_op jit(solution)/shard_map/ppermute | solution.py:303
  29.5 4.6 %collective-permute-start.4 = (f32[4,24,256]{2,1,0:T(8,128)S(1)}, f32[4,24,256]{2,1,0:T(8,128)S(1)}, u32[]{:S(2)}, u32[]{:S(2)}) collective-permute-start(f32[4,24,256]{2,1,0:T(8,128)S(1)} %pad_maximum_fusion.3), channel_id=1, source_target_pairs={{0,64},{4,68},{8,72},{12,76},{16,80},{20,84},{24,88},{28,92},{32,9... | collective-permute-start | bytes 294920 | tf_op jit(solution)/shard_map/ppermute | solution.py:303
  34.1 1.4 %collective-permute-start.9 = (f32[8,192]{1,0:T(8,128)S(1)}, f32[8,192]{1,0:T(8,128)S(1)}, u32[]{:S(2)}, u32[]{:S(2)}) collective-permute-start(f32[8,192]{1,0:T(8,128)S(1)} %pad_maximum_fusion.5), channel_id=1, source_target_pairs={{0,2},{1,3},{2,0},{3,1},{4,6},{5,7},{6,4},{7,5},{8,10},{9,11},{10,... | collective-permute-start | bytes 18440 | tf_op jit(solution)/shard_map/ppermute | solution.py:337
  35.5 1.8 %collective-permute-done.4.refs_4_ = f32[4,24,256]{2,1,0:T(8,128)S(1)} collective-permute-done((f32[4,24,256]{2,1,0:T(8,128)S(1)}, f32[4,24,256]{2,1,0:T(8,128)S(1)}, u32[]{:S(2)}, u32[]{:S(2)}) %collective-permute-start.4) | collective-permute-done | bytes 98336 | tf_op jit(solution)/shard_map/ppermute | solution.py:303
  37.9 5.7 %collective-permute-start.5 = (f32[4,24,256]{2,1,0:T(8,128)S(1)}, f32[4,24,256]{2,1,0:T(8,128)S(1)}, u32[]{:S(2)}, u32[]{:S(2)}) collective-permute-start(f32[4,24,256]{2,1,0:T(8,128)S(1)} %pad_maximum_fusion.4.refs_6_), channel_id=1, source_target_pairs={{0,192},{4,196},{8,200},{12,204},{16,208},{20,212},{24,216},{28,22... | collective-permute-start | bytes 294920 | tf_op jit(solution)/shard_map/ppermute | solution.py:303
  43.7 1.8 %convolution_add_fusion = f32[192,256]{1,0:T(8,128)} fusion(f32[192,256]{1,0:T(8,128)S(1)} %convolution_bitcast_fusion, f32[8,192]{1,0:T(8,128)S(1)} %collective-permute-done.9, f32[4,192]{1,0:T(4,128)S(1)} %collective-permute-done.8, f32[4,12,256]{2,1,0:T(8,128)} %constant.68.clone, s32[]{:T(128)S(6)} %select_n.114), kind=kOutput, calls=%fused_computation.1 | convolution fusion | flops 7129344 | bytes 418820 | tf_op jit(solution)/shard_map/dot_general | solution.py:344
  45.4 0.6 %copy-done.8 = f32[24,4,256]{2,1,0:T(4,128)} copy-done((f32[24,4,256]{2,1,0:T(4,128)}, f32[24,4,256]{2,1,0:T(4,128)S(1)}, u32[]{:S(2)}) %copy-start.8) | copy-done | bytes 98328
  46.1 0.6 %copy-done.9 = f32[24,4,256]{2,1,0:T(4,128)} copy-done((f32[24,4,256]{2,1,0:T(4,128)}, f32[24,4,256]{2,1,0:T(4,128)S(1)}, u32[]{:S(2)}) %copy-start.9) | copy-done | bytes 98328
  46.7 2.2 %near.1 = (f32[24,8,256]{2,1,0:T(8,128)}, f32[24,8,256]{2,1,0:T(8,128)}) custom-call(f32[24,8,256]{2,1,0:T(8,128)} %bitcast.21, f32[24,4,256]{2,1,0:T(4,128)} %copy-done.8, f32[24,4,256]{2,1,0:T(4,128)} %copy-done.9), custom_call_target="tpu_custom_call" | custom-call | tf_op jit(solution)/shard_map/near/pallas_call | solution.py:323
  48.9 0.6 %copy-done.7 = f32[4,24,256]{2,1,0:T(8,128)} copy-done((f32[4,24,256]{2,1,0:T(8,128)}, f32[4,24,256]{2,1,0:T(8,128)S(1)}, u32[]{:S(2)}) %copy-start.7) | copy-done | bytes 98328
  49.6 2.1 %far.1 = (f32[24,8,256]{2,1,0:T(8,128)}, f32[24,8,256]{2,1,0:T(8,128)}) custom-call(f32[7,4]{1,0:T(8,128)} %copy.8.coef_ref, f32[4,24,256]{2,1,0:T(8,128)} %copy-done.1, f32[4,24,256]{2,1,0:T(8,128)} %copy-done.2, f32[4,24,256]{2,1,0:T(8,128)} %copy-done.3, f32[4,24,256]{2,1,0:T(8,128)} %copy-done.4, f32[4,24,256]{2,1,0:T(8,128)} %copy-done.5, ...), custom_call_target="tpu_custom_call" | custom-call | tf_op jit(solution)/shard_map/far/pallas_call | solution.py:346
  (35 shorter events, 1.8 us)
Async XLA Ops:
  2.5 7.4 %collective-permute-start = (f32[4,24,256]{2,1,0:T(8,128)}, f32[4,24,256]{2,1,0:T(8,128)S(1)}, u32[]{:S(2)}, u32[]{:S(2)}) collective-permute-start(f32[4,24,256]{2,1,0:T(8,128)} %get-tuple-element.10), channel_id=1, source_target_pairs={{0,4},{4,0},{8,12},{12,8},{16,20},{20,16},{24,28},{28,24},{32,36},... | collective-permute-start | bytes 294920 | tf_op jit(solution)/shard_map/ppermute | solution.py:303
  3.3 42.1 %collective-permute-start.6 = (f32[24,4,256]{2,1,0:T(4,128)}, f32[24,4,256]{2,1,0:T(4,128)S(1)}, u32[]{:S(2)}, u32[]{:S(2)}) collective-permute-start(f32[24,4,256]{2,1,0:T(4,128)} %get-tuple-element.11), channel_id=1, source_target_pairs={{4,0},{8,4},{12,8},{16,12},{20,16},{24,20},{28,24},{32,28},{36,32}... | collective-permute-start | bytes 294920 | tf_op jit(solution)/shard_map/ppermute | solution.py:320
  4.5 40.9 %collective-permute-start.7 = (f32[24,4,256]{2,1,0:T(4,128)}, f32[24,4,256]{2,1,0:T(4,128)S(1)}, u32[]{:S(2)}, u32[]{:S(2)}) collective-permute-start(f32[24,4,256]{2,1,0:T(4,128)} %get-tuple-element.12), channel_id=1, source_target_pairs={{0,4},{4,8},{8,12},{12,16},{16,20},{20,24},{24,28},{28,32},{32,36}... | collective-permute-start | bytes 294920 | tf_op jit(solution)/shard_map/ppermute | solution.py:319
  9.8 1.0 %copy-start = (f32[3,8,8,256]{3,2,1,0:T(8,128)S(1)}, f32[3,8,8,256]{3,2,1,0:T(8,128)}, u32[]{:S(2)}) copy-start(f32[3,8,8,256]{3,2,1,0:T(8,128)} %param.5) | copy-start | bytes 589828
  9.8 0.9 %copy-start.1 = (f32[4,24,256]{2,1,0:T(8,128)}, f32[4,24,256]{2,1,0:T(8,128)S(1)}, u32[]{:S(2)}) copy-start(f32[4,24,256]{2,1,0:T(8,128)S(1)} %collective-permute-done.refs_0_) | copy-start | bytes 294916
  10.7 5.9 %collective-permute-start.1 = (f32[4,24,256]{2,1,0:T(8,128)S(1)}, f32[4,24,256]{2,1,0:T(8,128)S(1)}, u32[]{:S(2)}, u32[]{:S(2)}) collective-permute-start(f32[4,24,256]{2,1,0:T(8,128)S(1)} %pad_maximum_fusion), channel_id=1, source_target_pairs={{0,12},{4,8},{8,4},{12,0},{16,28},{20,24},{24,20},{28,16},{32,44},... | collective-permute-start | bytes 294920 | tf_op jit(solution)/shard_map/ppermute | solution.py:303
  11.7 22.3 %collective-permute-start.8 = (f32[4,192]{1,0:T(4,128)S(1)}, f32[4,192]{1,0:T(4,128)S(1)}, u32[]{:S(2)}, u32[]{:S(2)}) collective-permute-start(f32[4,192]{1,0:T(4,128)S(1)} %fusion.27), channel_id=1, source_target_pairs={{0,1},{1,0},{2,3},{3,2},{4,5},{5,4},{6,7},{7,6},{8,9},{9,8},{10,11... | collective-permute-start | bytes 9224 | tf_op jit(solution)/shard_map/ppermute | solution.py:335
  16.6 0.7 %copy-start.2 = (f32[4,24,256]{2,1,0:T(8,128)}, f32[4,24,256]{2,1,0:T(8,128)S(1)}, u32[]{:S(2)}) copy-start(f32[4,24,256]{2,1,0:T(8,128)S(1)} %collective-permute-done.1.refs_1_) | copy-start | bytes 294916
  17.3 6.2 %collective-permute-start.2 = (f32[4,24,256]{2,1,0:T(8,128)S(1)}, f32[4,24,256]{2,1,0:T(8,128)S(1)}, u32[]{:S(2)}, u32[]{:S(2)}) collective-permute-start(f32[4,24,256]{2,1,0:T(8,128)S(1)} %pad_maximum_fusion.1), channel_id=1, source_target_pairs={{0,16},{4,20},{8,24},{12,28},{16,0},{20,4},{24,8},{28,12},{32,48},... | collective-permute-start | bytes 294920 | tf_op jit(solution)/shard_map/ppermute | solution.py:303
  23.5 0.6 %copy-start.3 = (f32[4,24,256]{2,1,0:T(8,128)}, f32[4,24,256]{2,1,0:T(8,128)S(1)}, u32[]{:S(2)}) copy-start(f32[4,24,256]{2,1,0:T(8,128)S(1)} %collective-permute-done.2.refs_2_) | copy-start | bytes 294916
  24.2 4.7 %collective-permute-start.3 = (f32[4,24,256]{2,1,0:T(8,128)S(1)}, f32[4,24,256]{2,1,0:T(8,128)S(1)}, u32[]{:S(2)}, u32[]{:S(2)}) collective-permute-start(f32[4,24,256]{2,1,0:T(8,128)S(1)} %pad_maximum_fusion.2), channel_id=1, source_target_pairs={{0,32},{4,36},{8,40},{12,44},{16,48},{20,52},{24,56},{28,60},{32,0... | collective-permute-start | bytes 294920 | tf_op jit(solution)/shard_map/ppermute | solution.py:303
  28.9 0.6 %copy-start.4 = (f32[4,24,256]{2,1,0:T(8,128)}, f32[4,24,256]{2,1,0:T(8,128)S(1)}, u32[]{:S(2)}) copy-start(f32[4,24,256]{2,1,0:T(8,128)S(1)} %collective-permute-done.3.refs_3_) | copy-start | bytes 294916
  29.5 7.8 %collective-permute-start.4 = (f32[4,24,256]{2,1,0:T(8,128)S(1)}, f32[4,24,256]{2,1,0:T(8,128)S(1)}, u32[]{:S(2)}, u32[]{:S(2)}) collective-permute-start(f32[4,24,256]{2,1,0:T(8,128)S(1)} %pad_maximum_fusion.3), channel_id=1, source_target_pairs={{0,64},{4,68},{8,72},{12,76},{16,80},{20,84},{24,88},{28,92},{32,9... | collective-permute-start | bytes 294920 | tf_op jit(solution)/shard_map/ppermute | solution.py:303
  34.1 9.6 %collective-permute-start.9 = (f32[8,192]{1,0:T(8,128)S(1)}, f32[8,192]{1,0:T(8,128)S(1)}, u32[]{:S(2)}, u32[]{:S(2)}) collective-permute-start(f32[8,192]{1,0:T(8,128)S(1)} %pad_maximum_fusion.5), channel_id=1, source_target_pairs={{0,2},{1,3},{2,0},{3,1},{4,6},{5,7},{6,4},{7,5},{8,10},{9,11},{10,... | collective-permute-start | bytes 18440 | tf_op jit(solution)/shard_map/ppermute | solution.py:337
  37.3 0.6 %copy-start.5 = (f32[4,24,256]{2,1,0:T(8,128)}, f32[4,24,256]{2,1,0:T(8,128)S(1)}, u32[]{:S(2)}) copy-start(f32[4,24,256]{2,1,0:T(8,128)S(1)} %collective-permute-done.4.refs_4_) | copy-start | bytes 294916
  37.9 7.5 %copy-start.6 = (f32[4,24,256]{2,1,0:T(8,128)}, f32[4,24,256]{2,1,0:T(8,128)S(1)}, u32[]{:S(2)}) copy-start(f32[4,24,256]{2,1,0:T(8,128)S(1)} %pad_maximum_fusion.4.refs_6_) | copy-start | bytes 294916
  37.9 11.0 %collective-permute-start.5 = (f32[4,24,256]{2,1,0:T(8,128)S(1)}, f32[4,24,256]{2,1,0:T(8,128)S(1)}, u32[]{:S(2)}, u32[]{:S(2)}) collective-permute-start(f32[4,24,256]{2,1,0:T(8,128)S(1)} %pad_maximum_fusion.4.refs_6_), channel_id=1, source_target_pairs={{0,192},{4,196},{8,200},{12,204},{16,208},{20,212},{24,216},{28,22... | collective-permute-start | bytes 294920 | tf_op jit(solution)/shard_map/ppermute | solution.py:303
  45.4 0.6 %copy-start.8 = (f32[24,4,256]{2,1,0:T(4,128)}, f32[24,4,256]{2,1,0:T(4,128)S(1)}, u32[]{:S(2)}) copy-start(f32[24,4,256]{2,1,0:T(4,128)S(1)} %collective-permute-done.6.right_ref) | copy-start | bytes 294916
  46.1 0.6 %copy-start.9 = (f32[24,4,256]{2,1,0:T(4,128)}, f32[24,4,256]{2,1,0:T(4,128)S(1)}, u32[]{:S(2)}) copy-start(f32[24,4,256]{2,1,0:T(4,128)S(1)} %collective-permute-done.7.left_ref) | copy-start | bytes 294916
  48.9 0.6 %copy-start.7 = (f32[4,24,256]{2,1,0:T(8,128)}, f32[4,24,256]{2,1,0:T(8,128)S(1)}, u32[]{:S(2)}) copy-start(f32[4,24,256]{2,1,0:T(8,128)S(1)} %collective-permute-done.5.refs_5_) | copy-start | bytes 294916

commit v2 on v1

--- a/solution.py
+++ b/solution.py
@@ -263,6 +263,10 @@
             outs[which][n] = near[which][n] + a * from_left + b * from_right
 
 
+def in_vmem(x):
+    return pltpu.with_memory_space_constraint(x, pltpu.VMEM)
+
+
 def vmem(count):
     return [pl.BlockSpec(memory_space=pltpu.VMEM)] * count
 
@@ -286,9 +290,9 @@
     totals, first, last = pl.pallas_call(
         functools.partial(totals_kernel, weights),
         out_shape=(
-            jax.ShapeDtypeStruct((4, lines, width), f32),
-            jax.ShapeDtypeStruct((lines, REACH, width), f32),
-            jax.ShapeDtypeStruct((lines, REACH, width), f32),
+            pltpu.VMEM((4, lines, width), f32),
+            pltpu.VMEM((lines, REACH, width), f32),
+            pltpu.VMEM((lines, REACH, width), f32),
         ),
         in_specs=vmem(1),
         out_specs=tuple(vmem(3)),
@@ -322,11 +326,11 @@
     local, halo = circ_tables(cells)
     d_near, f_near = pl.pallas_call(
         functools.partial(near_kernel, local, halo),
-        out_shape=(jax.ShapeDtypeStruct(u.shape, f32),) * 2,
+        out_shape=(pltpu.VMEM(u.shape, f32),) * 2,
         in_specs=vmem(3),
         out_specs=tuple(vmem(2)),
         name="near",
-    )(u, right, left)
+    )(u, in_vmem(right), in_vmem(left))
 
     ax_local, ax_gather, ax_spread = axial_tables(width, ax_count)
     rows = u.reshape(lines * cells, width)
@@ -350,7 +354,7 @@
         out_specs=tuple(vmem(2)),
         scratch_shapes=[pltpu.VMEM((4, lines, width), f32)],
         name="far",
-    )(coef, *got, d_near, f_near)
+    )(coef, *[in_vmem(x) for x in got], in_vmem(d_near), in_vmem(f_near))
     shape = fields.shape
     return d_circ.reshape(shape), ax_out.reshape(shape), filtered.reshape(shape)
 

time: 52.1 us -> 45.1 us (0.87)
  local copies, waits for them, and re-layouts: 5.8 us -> 2.15 us
  Pallas kernels: 6.2 us -> 4.12 us
  other arithmetic: 0.98 us -> 0.15 us
    unnamed x20 -> x2, local copies, waits for them, and re-layouts: 4.43 us -> 0.79 us
    pallas_call x2, Pallas kernels: 4.06 us -> 2.56 us  [the longest x1 1.39 us: shards(): pl.pallas_call(functools.partial(near_kernel, local, halo), out_shape=(pl...]
    add x5, other arithmetic: 0.93 us -> 0.09 us  [shards(): own[v] * totals[v] + their[v] * other[v]]
    pallas_call x1, Pallas kernels: 2.14 us -> 1.57 us  [shards(): pl.pallas_call(functools.partial(far_kernel, rounds, roots), out_shape=(j...]
  transfers between devices with their start and end apart: 10 -> 10, of which waited for: 4 -> 5; matrix products, arithmetic and copies ran while one was open for 12% -> 12% of each run, Pallas kernels for 4% -> 3%
where the time goes in v2:
time: 45.1 us; the launch traced here: 44.8 us
  starting transfers between devices  19.5 us (43%)
  waiting for transfers between devices  14.1 us (31%)
  Pallas kernels  4.12 us (9%)
  matrix products  3.95 us (9%)
  local copies, waits for them, and re-layouts  2.15 us (5%)
  between operations  0.78 us (2%)
    ppermute x6, waiting for transfers between devices, shards(): lax.ppermute(totals, 'circ', [(i, i ^ masks[k]) for i in range(circ_count)])  14.1 us
    ppermute x6, starting transfers between devices, shards(): lax.ppermute(totals, 'circ', [(i, i ^ masks[k]) for i in range(circ_count)])  11.6 us
    ppermute x1, starting transfers between devices, shards(): left = lax.ppermute(last, 'circ', ring)  5.34 us
    dot_general x1, matrix products, shards(): lax.dot_general(ax_in, spread, (((0,), (0,)), ((), ())), precision=PRECISE)  1.76 us
    pallas_call x1, Pallas kernels, shards(): pl.pallas_call(functools.partial(far_kernel, rounds, roots), out_shape=(j...  1.57 us
    pallas_call x1, Pallas kernels, shards(): pl.pallas_call(functools.partial(near_kernel, local, halo), out_shape=(pl...  1.39 us
    ppermute x1, starting transfers between devices, shards(): far_side = lax.ppermute(pair, 'ax', [(i, i ^ 2) for i in range(ax_count)])  1.37 us
    squeeze x2, local copies, waits for them, and re-layouts, shards(): lax.dynamic_index_in_dim(jnp.asarray(table, f32), circ_place, 0, False)  1.36 us
  transfers between devices with their start and end apart: 10, of which 5 were waited for; matrix products, arithmetic and copies ran while one was open for 12% of the time, Pallas kernels for 3%

profile of v2, /device:TPU:54, one launch (start us, length us, event | category | flops | bytes accessed | tf_op | source)
XLA Modules:
  0.0 44.8 jit_solution(9159453890107191755)
XLA Ops:
  0.6 1.2 %totals.1 = (f32[4,24,256]{2,1,0:T(8,128)S(1)}, f32[24,4,256]{2,1,0:T(4,128)S(1)}, f32[24,4,256]{2,1,0:T(4,128)S(1)}) custom-call(f32[24,8,256]{2,1,0:T(8,128)} %bitcast.20), custom_call_target="tpu_custom_call" | custom-call | tf_op jit(solution)/shard_map/totals/pallas_call | solution.py:290
  1.8 0.9 %collective-permute-start = (f32[4,24,256]{2,1,0:T(8,128)S(1)}, f32[4,24,256]{2,1,0:T(8,128)S(1)}, u32[]{:S(2)}, u32[]{:S(2)}) collective-permute-start(f32[4,24,256]{2,1,0:T(8,128)S(1)} %get-tuple-element.10), channel_id=1, source_target_pairs={{0,4},{4,0},{8,12},{12,8},{16,20},{20,16},{24,28},{28,24},{32,36},... | collective-permute-start | bytes 294920 | tf_op jit(solution)/shard_map/ppermute | solution.py:307
  2.7 1.2 %collective-permute-start.6 = (f32[24,4,256]{2,1,0:T(4,128)S(1)}, f32[24,4,256]{2,1,0:T(4,128)S(1)}, u32[]{:S(2)}, u32[]{:S(2)}) collective-permute-start(f32[24,4,256]{2,1,0:T(4,128)S(1)} %get-tuple-element.11), channel_id=1, source_target_pairs={{4,0},{8,4},{12,8},{16,12},{20,16},{24,20},{28,24},{32,28},{36,32}... | collective-permute-start | bytes 294920 | tf_op jit(solution)/shard_map/ppermute | solution.py:324
  3.9 5.3 %collective-permute-start.7 = (f32[24,4,256]{2,1,0:T(4,128)S(1)}, f32[24,4,256]{2,1,0:T(4,128)S(1)}, u32[]{:S(2)}, u32[]{:S(2)}) collective-permute-start(f32[24,4,256]{2,1,0:T(4,128)S(1)} %get-tuple-element.12), channel_id=1, source_target_pairs={{0,4},{4,8},{8,12},{12,16},{16,20},{20,24},{24,28},{28,32},{32,36}... | collective-permute-start | bytes 294920 | tf_op jit(solution)/shard_map/ppermute | solution.py:323
  9.3 0.1 collective-permute-start.1
  9.4 0.8 %copy-done = f32[3,8,8,256]{3,2,1,0:T(8,128)S(1)} copy-done((f32[3,8,8,256]{3,2,1,0:T(8,128)S(1)}, f32[3,8,8,256]{3,2,1,0:T(8,128)}, u32[]{:S(2)}) %copy-start) | copy-done | bytes 196632
  10.2 0.9 %fusion.27 = f32[4,192]{1,0:T(4,128)S(1)} fusion(f32[192,256]{1,0:T(8,128)S(1)} %bitcast.22, f32[4,4,256]{2,1,0:T(4,128)} %constant.67.clone, s32[]{:T(128)S(6)} %select_n.114), kind=kOutput, calls=%fused_computation.55 | convolution fusion | flops 2359296 | bytes 203780 | tf_op jit(solution)/shard_map/dot_general | solution.py:338
  11.1 0.1 collective-permute-start.8
  11.1 4.1 %collective-permute-done.1.refs_1_ = f32[4,24,256]{2,1,0:T(8,128)S(1)} collective-permute-done((f32[4,24,256]{2,1,0:T(8,128)S(1)}, f32[4,24,256]{2,1,0:T(8,128)S(1)}, u32[]{:S(2)}, u32[]{:S(2)}) %collective-permute-start.1) | collective-permute-done | bytes 98336 | tf_op jit(solution)/shard_map/ppermute | solution.py:307
  15.2 0.1 collective-permute-start.2
  15.3 1.3 %convolution_bitcast_fusion = f32[192,256]{1,0:T(8,128)S(1)} fusion(f32[192,256]{1,0:T(8,128)S(1)} %bitcast.23, f32[4,256,256]{2,1,0:T(8,128)} %constant.69.clone, s32[]{:T(128)S(6)} %select_n.114), kind=kOutput, calls=%fused_computation | convolution fusion | flops 150994944 | bytes 655364 | tf_op jit(solution)/shard_map/dot_general | solution.py:347
  16.7 4.8 %collective-permute-done.2.refs_2_ = f32[4,24,256]{2,1,0:T(8,128)S(1)} collective-permute-done((f32[4,24,256]{2,1,0:T(8,128)S(1)}, f32[4,24,256]{2,1,0:T(8,128)S(1)}, u32[]{:S(2)}, u32[]{:S(2)}) %collective-permute-start.2) | collective-permute-done | bytes 98336 | tf_op jit(solution)/shard_map/ppermute | solution.py:307
  21.5 0.2 collective-permute-start.3
  21.7 0.7 %dynamic-slice_bitcast_fusion = f32[7,4]{0,1:T(4,128)S(1)} fusion(f32[64,7,4]{1,2,0:T(4,128)} %constant.66.clone, s32[]{:T(128)S(6)} %select_n.93), kind=kLoop, calls=%fused_computation.58 | loop fusion | bytes 228 | tf_op jit(solution)/shard_map/jit(dynamic_index_in_dim)/squeeze | solution.py:303
  22.4 0.7 %copy.8.coef_ref = f32[7,4]{1,0:T(8,128)} copy(f32[7,4]{0,1:T(4,128)S(1)} %dynamic-slice_bitcast_fusion) | data formatting | bytes 224 | tf_op jit(solution)/shard_map/jit(dynamic_index_in_dim)/squeeze | solution.py:303
  23.0 3.1 %collective-permute-done.3.refs_3_ = f32[4,24,256]{2,1,0:T(8,128)S(1)} collective-permute-done((f32[4,24,256]{2,1,0:T(8,128)S(1)}, f32[4,24,256]{2,1,0:T(8,128)S(1)}, u32[]{:S(2)}, u32[]{:S(2)}) %collective-permute-start.3) | collective-permute-done | bytes 98336 | tf_op jit(solution)/shard_map/ppermute | solution.py:307
  26.2 4.7 %collective-permute-start.4 = (f32[4,24,256]{2,1,0:T(8,128)S(1)}, f32[4,24,256]{2,1,0:T(8,128)S(1)}, u32[]{:S(2)}, u32[]{:S(2)}) collective-permute-start(f32[4,24,256]{2,1,0:T(8,128)S(1)} %pad_maximum_fusion.3), channel_id=1, source_target_pairs={{0,64},{4,68},{8,72},{12,76},{16,80},{20,84},{24,88},{28,92},{32,9... | collective-permute-start | bytes 294920 | tf_op jit(solution)/shard_map/ppermute | solution.py:307
  30.9 1.4 %collective-permute-start.9 = (f32[8,192]{1,0:T(8,128)S(1)}, f32[8,192]{1,0:T(8,128)S(1)}, u32[]{:S(2)}, u32[]{:S(2)}) collective-permute-start(f32[8,192]{1,0:T(8,128)S(1)} %pad_maximum_fusion.5), channel_id=1, source_target_pairs={{0,2},{1,3},{2,0},{3,1},{4,6},{5,7},{6,4},{7,5},{8,10},{9,11},{10,... | collective-permute-start | bytes 18440 | tf_op jit(solution)/shard_map/ppermute | solution.py:341
  32.3 1.8 %collective-permute-done.4.refs_4_ = f32[4,24,256]{2,1,0:T(8,128)S(1)} collective-permute-done((f32[4,24,256]{2,1,0:T(8,128)S(1)}, f32[4,24,256]{2,1,0:T(8,128)S(1)}, u32[]{:S(2)}, u32[]{:S(2)}) %collective-permute-start.4) | collective-permute-done | bytes 98336 | tf_op jit(solution)/shard_map/ppermute | solution.py:307
  34.1 5.6 %collective-permute-start.5 = (f32[4,24,256]{2,1,0:T(8,128)S(1)}, f32[4,24,256]{2,1,0:T(8,128)S(1)}, u32[]{:S(2)}, u32[]{:S(2)}) collective-permute-start(f32[4,24,256]{2,1,0:T(8,128)S(1)} %pad_maximum_fusion.4.refs_6_), channel_id=1, source_target_pairs={{0,192},{4,196},{8,200},{12,204},{16,208},{20,212},{24,216},{28,22... | collective-permute-start | bytes 294920 | tf_op jit(solution)/shard_map/ppermute | solution.py:307
  39.7 1.8 %convolution_add_fusion = f32[192,256]{1,0:T(8,128)} fusion(f32[192,256]{1,0:T(8,128)S(1)} %convolution_bitcast_fusion, f32[8,192]{1,0:T(8,128)S(1)} %collective-permute-done.9, f32[4,192]{1,0:T(4,128)S(1)} %collective-permute-done.8, f32[4,12,256]{2,1,0:T(8,128)} %constant.68.clone, s32[]{:T(128)S(6)} %select_n.114), kind=kOutput, calls=%fused_computation.1 | convolution fusion | flops 7129344 | bytes 418820 | tf_op jit(solution)/shard_map/dot_general | solution.py:348
  41.5 1.4 %near.1 = (f32[24,8,256]{2,1,0:T(8,128)S(1)}, f32[24,8,256]{2,1,0:T(8,128)S(1)}) custom-call(f32[24,8,256]{2,1,0:T(8,128)} %bitcast.21, f32[24,4,256]{2,1,0:T(4,128)S(1)} %collective-permute-done.6.right_ref, f32[24,4,256]{2,1,0:T(4,128)S(1)} %collective-permute-done.7.left_ref), custom_call_target="tpu_custom_call" | custom-call | tf_op jit(solution)/shard_map/near/pallas_call | solution.py:327
  42.9 0.3 collective-permute-done.5.refs_5_
  43.2 1.6 %far.1 = (f32[24,8,256]{2,1,0:T(8,128)}, f32[24,8,256]{2,1,0:T(8,128)}) custom-call(f32[7,4]{1,0:T(8,128)} %copy.8.coef_ref, f32[4,24,256]{2,1,0:T(8,128)S(1)} %collective-permute-done.refs_0_, f32[4,24,256]{2,1,0:T(8,128)S(1)} %collective-permute-done.1.refs_1_, f32[4,24,256]{2,1,0:T(8,128)S(1)} %collective-permute-done.2.refs_2_, ...), custom_call_target="tpu_custom_call" | custom-call | tf_op jit(solution)/shard_map/far/pallas_call | solution.py:350
  (17 shorter events, 0.2 us)
Async XLA Ops:
  1.8 7.5 %collective-permute-start = (f32[4,24,256]{2,1,0:T(8,128)S(1)}, f32[4,24,256]{2,1,0:T(8,128)S(1)}, u32[]{:S(2)}, u32[]{:S(2)}) collective-permute-start(f32[4,24,256]{2,1,0:T(8,128)S(1)} %get-tuple-element.10), channel_id=1, source_target_pairs={{0,4},{4,0},{8,12},{12,8},{16,20},{20,16},{24,28},{28,24},{32,36},... | collective-permute-start | bytes 294920 | tf_op jit(solution)/shard_map/ppermute | solution.py:307
  2.7 38.8 %collective-permute-start.6 = (f32[24,4,256]{2,1,0:T(4,128)S(1)}, f32[24,4,256]{2,1,0:T(4,128)S(1)}, u32[]{:S(2)}, u32[]{:S(2)}) collective-permute-start(f32[24,4,256]{2,1,0:T(4,128)S(1)} %get-tuple-element.11), channel_id=1, source_target_pairs={{4,0},{8,4},{12,8},{16,12},{20,16},{24,20},{28,24},{32,28},{36,32}... | collective-permute-start | bytes 294920 | tf_op jit(solution)/shard_map/ppermute | solution.py:324
  3.9 37.6 %collective-permute-start.7 = (f32[24,4,256]{2,1,0:T(4,128)S(1)}, f32[24,4,256]{2,1,0:T(4,128)S(1)}, u32[]{:S(2)}, u32[]{:S(2)}) collective-permute-start(f32[24,4,256]{2,1,0:T(4,128)S(1)} %get-tuple-element.12), channel_id=1, source_target_pairs={{0,4},{4,8},{8,12},{12,16},{16,20},{20,24},{24,28},{28,32},{32,36}... | collective-permute-start | bytes 294920 | tf_op jit(solution)/shard_map/ppermute | solution.py:323
  9.3 0.9 %copy-start = (f32[3,8,8,256]{3,2,1,0:T(8,128)S(1)}, f32[3,8,8,256]{3,2,1,0:T(8,128)}, u32[]{:S(2)}) copy-start(f32[3,8,8,256]{3,2,1,0:T(8,128)} %param.5) | copy-start | bytes 589828
  9.3 5.9 %collective-permute-start.1 = (f32[4,24,256]{2,1,0:T(8,128)S(1)}, f32[4,24,256]{2,1,0:T(8,128)S(1)}, u32[]{:S(2)}, u32[]{:S(2)}) collective-permute-start(f32[4,24,256]{2,1,0:T(8,128)S(1)} %pad_maximum_fusion), channel_id=1, source_target_pairs={{0,12},{4,8},{8,4},{12,0},{16,28},{20,24},{24,20},{28,16},{32,44},... | collective-permute-start | bytes 294920 | tf_op jit(solution)/shard_map/ppermute | solution.py:307
  11.1 19.8 %collective-permute-start.8 = (f32[4,192]{1,0:T(4,128)S(1)}, f32[4,192]{1,0:T(4,128)S(1)}, u32[]{:S(2)}, u32[]{:S(2)}) collective-permute-start(f32[4,192]{1,0:T(4,128)S(1)} %fusion.27), channel_id=1, source_target_pairs={{0,1},{1,0},{2,3},{3,2},{4,5},{5,4},{6,7},{7,6},{8,9},{9,8},{10,11... | collective-permute-start | bytes 9224 | tf_op jit(solution)/shard_map/ppermute | solution.py:339
  15.2 6.2 %collective-permute-start.2 = (f32[4,24,256]{2,1,0:T(8,128)S(1)}, f32[4,24,256]{2,1,0:T(8,128)S(1)}, u32[]{:S(2)}, u32[]{:S(2)}) collective-permute-start(f32[4,24,256]{2,1,0:T(8,128)S(1)} %pad_maximum_fusion.1), channel_id=1, source_target_pairs={{0,16},{4,20},{8,24},{12,28},{16,0},{20,4},{24,8},{28,12},{32,48},... | collective-permute-start | bytes 294920 | tf_op jit(solution)/shard_map/ppermute | solution.py:307
  21.5 4.7 %collective-permute-start.3 = (f32[4,24,256]{2,1,0:T(8,128)S(1)}, f32[4,24,256]{2,1,0:T(8,128)S(1)}, u32[]{:S(2)}, u32[]{:S(2)}) collective-permute-start(f32[4,24,256]{2,1,0:T(8,128)S(1)} %pad_maximum_fusion.2), channel_id=1, source_target_pairs={{0,32},{4,36},{8,40},{12,44},{16,48},{20,52},{24,56},{28,60},{32,0... | collective-permute-start | bytes 294920 | tf_op jit(solution)/shard_map/ppermute | solution.py:307
  26.2 7.8 %collective-permute-start.4 = (f32[4,24,256]{2,1,0:T(8,128)S(1)}, f32[4,24,256]{2,1,0:T(8,128)S(1)}, u32[]{:S(2)}, u32[]{:S(2)}) collective-permute-start(f32[4,24,256]{2,1,0:T(8,128)S(1)} %pad_maximum_fusion.3), channel_id=1, source_target_pairs={{0,64},{4,68},{8,72},{12,76},{16,80},{20,84},{24,88},{28,92},{32,9... | collective-permute-start | bytes 294920 | tf_op jit(solution)/shard_map/ppermute | solution.py:307
  30.9 8.8 %collective-permute-start.9 = (f32[8,192]{1,0:T(8,128)S(1)}, f32[8,192]{1,0:T(8,128)S(1)}, u32[]{:S(2)}, u32[]{:S(2)}) collective-permute-start(f32[8,192]{1,0:T(8,128)S(1)} %pad_maximum_fusion.5), channel_id=1, source_target_pairs={{0,2},{1,3},{2,0},{3,1},{4,6},{5,7},{6,4},{7,5},{8,10},{9,11},{10,... | collective-permute-start | bytes 18440 | tf_op jit(solution)/shard_map/ppermute | solution.py:341
  34.1 9.1 %collective-permute-start.5 = (f32[4,24,256]{2,1,0:T(8,128)S(1)}, f32[4,24,256]{2,1,0:T(8,128)S(1)}, u32[]{:S(2)}, u32[]{:S(2)}) collective-permute-start(f32[4,24,256]{2,1,0:T(8,128)S(1)} %pad_maximum_fusion.4.refs_6_), channel_id=1, source_target_pairs={{0,192},{4,196},{8,200},{12,204},{16,208},{20,212},{24,216},{28,22... | collective-permute-start | bytes 294920 | tf_op jit(solution)/shard_map/ppermute | solution.py:307

commit v3 on v2

--- a/solution.py
+++ b/solution.py
@@ -9,12 +9,15 @@
 from jax.experimental.pallas import tpu as pltpu
 from jax.sharding import PartitionSpec as P
 
+
 DERIV_NEAR = 14.0 / 9.0
 DERIV_FAR = 1.0 / 9.0
 ALPHA_DERIV = 1.0 / 3.0
 ALPHA_FILTER = 0.4999
 PRECISE = lax.Precision.HIGHEST
 REACH = 4
+CHUNKS = 4
+GROUP = 4
 
 
 def filter_terms(coupling):
@@ -73,9 +76,11 @@
     return local, halo
 
 
-def carry_tables(cells, count):
+def carry_tables(cells, count, group):
+    first = group.bit_length() - 1
     rounds = count.bit_length() - 1
-    table = np.zeros((count, rounds + 1, 4))
+    later = rounds - first
+    table = np.zeros((count, group - 1 + later + 1, 4))
     merge = np.zeros((rounds, 2))
     for which, (coupling, stencil) in enumerate(stencils()):
         root, _, right, left = line_kernel(coupling, stencil)
@@ -84,23 +89,27 @@
         for k in range(rounds):
             merge[k, which] = step ** (1 << k)
         for p in range(count):
-            for k in range(rounds):
-                size = 1 << k
+            rows = table[p, :, 2 * which : 2 * which + 2]
+            for m in range(1, group):
+                q = p ^ m
+                if q < p:
+                    rows[m - 1, 0] = right * step ** (p - q - 1)
+                else:
+                    rows[m - 1, 1] = left * step ** (q - p - 1)
+            for k in range(first, rounds):
                 start = (p >> k) << k
-                end = start + size - 1
+                end = start + (1 << k) - 1
                 last = k == rounds - 1
+                slot = group - 1 + k - first + (1 if last else 0)
                 factor = wrap if last else 1.0
-                if (p >> k) & 1:
-                    table[p, k, 2 * which] = right * factor * step ** (p - start)
-                    if last:
-                        table[p, k, 2 * which + 1] = left * factor * step ** (count - 1 - p)
-                else:
-                    table[p, k, 2 * which + 1] = left * factor * step ** (end - p)
-                    if last:
-                        table[p, k, 2 * which] = right * factor * step**p
+                upper = (p >> k) & 1
+                if upper or last:
+                    rows[slot, 0] = right * factor * step ** (p - start if upper else p)
+                if not upper or last:
+                    rows[slot, 1] = left * factor * step ** (count - 1 - p if upper else end - p)
                 if last:
-                    table[p, rounds, 2 * which] = right * wrap * step ** (p + count - 1 - end)
-                    table[p, rounds, 2 * which + 1] = left * wrap * step ** (start + count - 1 - p)
+                    rows[slot - 1, 0] = right * wrap * step ** (p + count - 1 - end)
+                    rows[slot - 1, 1] = left * wrap * step ** (start + count - 1 - p)
     return table, merge
 
 
@@ -205,20 +214,42 @@
     return out
 
 
-def totals_kernel(weights, u_ref, s_ref, first_ref, last_ref):
+def totals_kernel(weights, u_hbm, s_ref, u_ref, sems):
     lines, cells, width = u_ref.shape
+    chunk = lines // CHUNKS
+    copies = []
+    for c in range(CHUNKS):
+        part = pl.ds(c * chunk, chunk)
+        copies.append(pltpu.make_async_copy(u_hbm.at[part], u_ref.at[part], sems.at[c]))
+        copies[-1].start()
     w = [by_row(weights[v], (cells, width)) for v in range(4)]
+    for c in range(CHUNKS):
+        copies[c].wait()
+        for n in range(c * chunk, (c + 1) * chunk):
+            un = u_ref[n]
+            for v in range(4):
+                s_ref[v, n : n + 1, :] = jnp.sum(un * w[v], axis=0, keepdims=True)
+
+
+def edges_kernel(u_ref, first_ref, last_ref):
+    lines, cells, _ = u_ref.shape
     for n in range(lines):
         un = u_ref[n]
-        for v in range(4):
-            s_ref[v, n : n + 1, :] = jnp.sum(un * w[v], axis=0, keepdims=True)
         first_ref[n] = un[:REACH]
         last_ref[n] = un[cells - REACH :]
 
 
-def near_kernel(local, halo, u_ref, right_ref, left_ref, d_ref, f_ref):
+def near_kernel(local, halo, count, roots, coef_ref, u_ref, right_ref, left_ref, *refs):
+    got = refs[:count]
+    d_ref, f_ref, tile_ref, lr = refs[count:]
     lines, cells, width = u_ref.shape
     outs = (d_ref, f_ref)
+    for v in range(4):
+        total = got[0][v] * coef_ref[0, v]
+        for k in range(1, count):
+            total = total + got[k][v] * coef_ref[k, v]
+        lr[v] = total
+        tile_ref[v] = jnp.full(tile_ref.shape[1:], coef_ref[count, v], jnp.float32)
     diag = {}
     for name, table in (("local", local), ("halo", halo)):
         for which in range(2):
@@ -226,10 +257,15 @@
                 values = [table[which, i, (i - s) % cells] for i in range(cells)]
                 if np.any(np.asarray(values) != 0.0):
                     diag[name, which, s] = by_row(values, (cells, width))
+    ramps = ramp_rows(roots, cells, width)
     for n in range(lines):
         un = u_ref[n]
         hn = jnp.concatenate([right_ref[n], left_ref[n]], axis=0)
-        acc = [None, None]
+        acc = [
+            ramps[2 * w] * jnp.broadcast_to(lr[2 * w, n : n + 1, :], (cells, width))
+            + ramps[2 * w + 1] * jnp.broadcast_to(lr[2 * w + 1, n : n + 1, :], (cells, width))
+            for w in range(2)
+        ]
         for name, value in (("local", un), ("halo", hn)):
             for s in range(cells):
                 used = [w for w in range(2) if (name, w, s) in diag]
@@ -237,30 +273,44 @@
                     continue
                 turned = pltpu.roll(value, s, 0) if s else value
                 for w in used:
-                    term = turned * diag[name, w, s]
-                    acc[w] = term if acc[w] is None else acc[w] + term
+                    acc[w] = acc[w] + turned * diag[name, w, s]
         for w in range(2):
             outs[w][n] = acc[w]
 
 
-def far_kernel(rounds, roots, coef_ref, *refs):
-    got = refs[: rounds + 1]
-    d_near, f_near, d_ref, f_ref, lr = refs[rounds + 1 :]
+def ramp_rows(roots, cells, width):
+    out = []
+    for root in roots:
+        out.append(by_row([root ** (i + 1) for i in range(cells)], (cells, width)))
+        out.append(by_row([root ** (cells - i) for i in range(cells)], (cells, width)))
+    return out
+
+
+def far_kernel(roots, tile_ref, got, d_near, f_near, d_hbm, f_hbm, lr, done, sems):
     lines, cells, width = d_near.shape
+    chunk = lines // CHUNKS
+    ramps = ramp_rows(roots, cells, width)
+    near = (d_near, f_near)
+    hbm = (d_hbm, f_hbm)
     for v in range(4):
-        total = got[0][v] * coef_ref[0, v]
-        for k in range(1, rounds + 1):
-            total = total + got[k][v] * coef_ref[k, v]
-        lr[v] = total
-    near = (d_near, f_near)
-    outs = (d_ref, f_ref)
-    for which in range(2):
-        a = by_row([roots[which] ** (i + 1) for i in range(cells)], (cells, width))
-        b = by_row([roots[which] ** (cells - i) for i in range(cells)], (cells, width))
-        for n in range(lines):
-            from_left = jnp.broadcast_to(lr[2 * which, n : n + 1, :], (cells, width))
-            from_right = jnp.broadcast_to(lr[2 * which + 1, n : n + 1, :], (cells, width))
-            outs[which][n] = near[which][n] + a * from_left + b * from_right
+        for n in range(0, lines, 8):
+            lr[v, n : n + 8] = got[v, n : n + 8] * tile_ref[v]
+    copies = []
+    for c in range(CHUNKS):
+        part = pl.ds(c * chunk, chunk)
+        for w in range(2):
+            for n in range(c * chunk, (c + 1) * chunk):
+                from_left = jnp.broadcast_to(lr[2 * w, n : n + 1, :], (cells, width))
+                from_right = jnp.broadcast_to(lr[2 * w + 1, n : n + 1, :], (cells, width))
+                done[w, n] = (
+                    near[w][n] + ramps[2 * w] * from_left + ramps[2 * w + 1] * from_right
+                )
+            copies.append(
+                pltpu.make_async_copy(done.at[w, part], hbm[w].at[part], sems.at[w, c])
+            )
+            copies[-1].start()
+    for copy in copies:
+        copy.wait()
 
 
 def in_vmem(x):
@@ -287,50 +337,78 @@
     for which, root in enumerate(roots):
         weights[2 * which] = root ** (cells - 1.0 - np.arange(cells))
         weights[2 * which + 1] = root ** (1.0 * np.arange(cells))
-    totals, first, last = pl.pallas_call(
+    totals, u = pl.pallas_call(
         functools.partial(totals_kernel, weights),
-        out_shape=(
-            pltpu.VMEM((4, lines, width), f32),
-            pltpu.VMEM((lines, REACH, width), f32),
-            pltpu.VMEM((lines, REACH, width), f32),
-        ),
-        in_specs=vmem(1),
-        out_specs=tuple(vmem(3)),
+        out_shape=(pltpu.VMEM((4, lines, width), f32), pltpu.VMEM(u.shape, f32)),
+        in_specs=[pl.BlockSpec(memory_space=pl.ANY)],
+        out_specs=tuple(vmem(2)),
+        scratch_shapes=[pltpu.SemaphoreType.DMA((CHUNKS,))],
         name="totals",
     )(u)
 
-    table, merge = carry_tables(cells, circ_count)
+    table, merge = carry_tables(cells, circ_count, GROUP)
+    steps = [root**cells for root in roots]
+    one = jnp.float32(1.0)
+    got = []
+    members = [totals]
+    for m in range(1, GROUP):
+        members.append(lax.ppermute(totals, "circ", [(i, i ^ m) for i in range(circ_count)]))
+    got += members[1:]
+    place = circ_place % GROUP
+    sums = []
+    for v in range(4):
+        total = None
+        for m in range(GROUP):
+            weights = [steps[v // 2] ** ((p ^ m) if v % 2 else GROUP - 1 - (p ^ m)) for p in range(GROUP)]
+            weight = jnp.float32(weights[0])
+            for p in range(1, GROUP):
+                weight = jnp.where(place == p, jnp.float32(weights[p]), weight)
+            term = weight * members[m][v]
+            total = term if total is None else total + term
+        sums.append(total)
+    totals = jnp.stack(sums)
+    masks = {2: 4, 3: 8, 4: 16, 5: 48}
+    for k in range(GROUP.bit_length() - 1, rounds):
+        other = lax.ppermute(totals, "circ", [(i, i ^ masks[k]) for i in range(circ_count)])
+        if k == rounds - 1:
+            got += [totals, other]
+            break
+        got.append(other)
+        on_right = ((circ_place >> k) & 1) == 1
+        new = []
+        for v in range(4):
+            g = jnp.float32(merge[k, v // 2])
+            grows = on_right if v % 2 else jnp.logical_not(on_right)
+            own = jnp.where(grows, g, one)
+            their = jnp.where(grows, one, g)
+            new.append(own * totals[v] + their * other[v])
+        totals = jnp.stack(new)
     coef = lax.dynamic_index_in_dim(jnp.asarray(table, f32), circ_place, 0, False)
-    masks = [1, 3, 4, 8, 16, 48]
-    got = []
-    for k in range(rounds):
-        other = lax.ppermute(totals, "circ", [(i, i ^ masks[k]) for i in range(circ_count)])
-        got.append(other)
-        if k < rounds - 1:
-            on_right = ((circ_place >> k) & 1) == 1
-            grow = [float(merge[k, 0]), float(merge[k, 1])]
-            own, their = [], []
-            for which in range(2):
-                one = jnp.float32(1.0)
-                g = jnp.float32(grow[which])
-                own += [jnp.where(on_right, one, g), jnp.where(on_right, g, one)]
-                their += [jnp.where(on_right, g, one), jnp.where(on_right, one, g)]
-            totals = jnp.stack([own[v] * totals[v] + their[v] * other[v] for v in range(4)])
-    got.append(totals)
-
+
+    u_near = in_vmem(u)
+    first, last = pl.pallas_call(
+        edges_kernel,
+        out_shape=(pltpu.VMEM((lines, REACH, width), f32),) * 2,
+        in_specs=vmem(1),
+        out_specs=tuple(vmem(2)),
+        name="edges",
+    )(u_near)
     ring = [(i, (i + 1) % circ_count) for i in range(circ_count)]
     gnir = [(j, i) for i, j in ring]
     left = lax.ppermute(last, "circ", ring)
     right = lax.ppermute(first, "circ", gnir)
 
     local, halo = circ_tables(cells)
-    d_near, f_near = pl.pallas_call(
-        functools.partial(near_kernel, local, halo),
-        out_shape=(pltpu.VMEM(u.shape, f32),) * 2,
-        in_specs=vmem(3),
-        out_specs=tuple(vmem(2)),
+    smem = [pl.BlockSpec(memory_space=pltpu.SMEM)]
+    carries = [in_vmem(x) for x in got[:-1]]
+    d_near, f_near, tile = pl.pallas_call(
+        functools.partial(near_kernel, local, halo, len(carries), roots),
+        out_shape=(pltpu.VMEM(u.shape, f32),) * 2 + (pltpu.VMEM((4, 8, width), f32),),
+        in_specs=smem + vmem(3 + len(carries)),
+        out_specs=tuple(vmem(3)),
+        scratch_shapes=[pltpu.VMEM((4, lines, width), f32)],
         name="near",
-    )(u, in_vmem(right), in_vmem(left))
+    )(coef, u_near, in_vmem(right), in_vmem(left), *carries)
 
     ax_local, ax_gather, ax_spread = axial_tables(width, ax_count)
     rows = u.reshape(lines * cells, width)
@@ -339,28 +417,33 @@
     near_side = lax.ppermute(sent, "ax", [(i, i ^ 1) for i in range(ax_count)])
     pair = jnp.concatenate([sent, near_side], axis=0)
     far_side = lax.ppermute(pair, "ax", [(i, i ^ 2) for i in range(ax_count)])
+    square = lax.dynamic_index_in_dim(jnp.asarray(ax_local.swapaxes(1, 2), f32), ax_place, 0, False)
+    ax_out = jnp.dot(rows, square, precision=PRECISE)
     order = np.asarray([[p ^ 1, p ^ 2, p ^ 3] for p in range(ax_count)])
     spread = np.stack([ax_spread[p][order[p]].reshape(12, width) for p in range(ax_count)])
     spread = lax.dynamic_index_in_dim(jnp.asarray(spread, f32), ax_place, 0, False)
-    square = lax.dynamic_index_in_dim(jnp.asarray(ax_local.swapaxes(1, 2), f32), ax_place, 0, False)
     ax_in = jnp.concatenate([near_side, far_side], axis=0)
-    ax_out = jnp.dot(rows, square, precision=PRECISE)
     ax_out = ax_out + lax.dot_general(ax_in, spread, (((0,), (0,)), ((), ())), precision=PRECISE)
 
     d_circ, filtered = pl.pallas_call(
-        functools.partial(far_kernel, rounds, roots),
+        functools.partial(far_kernel, roots),
         out_shape=(jax.ShapeDtypeStruct(u.shape, f32),) * 2,
-        in_specs=[pl.BlockSpec(memory_space=pltpu.SMEM)] + vmem(rounds + 3),
-        out_specs=tuple(vmem(2)),
-        scratch_shapes=[pltpu.VMEM((4, lines, width), f32)],
+        in_specs=vmem(4),
+        out_specs=(pl.BlockSpec(memory_space=pl.ANY),) * 2,
+        scratch_shapes=[
+            pltpu.VMEM((4, lines, width), f32),
+            pltpu.VMEM((2, *u.shape), f32),
+            pltpu.SemaphoreType.DMA((2, CHUNKS)),
+        ],
         name="far",
-    )(coef, *[in_vmem(x) for x in got], in_vmem(d_near), in_vmem(f_near))
+    )(in_vmem(tile), in_vmem(got[-1]), in_vmem(d_near), in_vmem(f_near))
     shape = fields.shape
     return d_circ.reshape(shape), ax_out.reshape(shape), filtered.reshape(shape)
 
 
 def solution(mesh):
     spec = P(None, None, "circ", "ax")
+
     return jax.shard_map(
         shards, mesh=mesh, in_specs=(spec,), out_specs=(spec, spec, spec), check_vma=False
     )

time: 45.1 us -> 44.2 us (0.980)
  the two profiles are of different devices: /device:TPU:54 before, /device:TPU:8 now
where the time goes in v3:
time: 44.2 us; the launch traced here: 43.9 us
  starting transfers between devices  18.7 us (42%)
  waiting for transfers between devices  15.6 us (35%)
  matrix products  3.95 us (9%)
  Pallas kernels  3.19 us (7%)
  local copies, waits for them, and re-layouts  1.36 us (3%)
  between operations  0.87 us (2%)
    ppermute x4, waiting for transfers between devices, shards(): lax.ppermute(totals, 'circ', [(i, i ^ masks[k]) for i in range(circ_count)])  15.6 us
    ppermute x1, starting transfers between devices, shards(): right = lax.ppermute(first, 'circ', gnir)  9.86 us
    ppermute x3, starting transfers between devices, shards(): lax.ppermute(totals, 'circ', [(i, i ^ m) for i in range(circ_count)])  4.79 us
    ppermute x4, starting transfers between devices, shards(): lax.ppermute(totals, 'circ', [(i, i ^ masks[k]) for i in range(circ_count)])  2.57 us
    dot_general x1, matrix products, shards(): lax.dot_general(ax_in, spread, (((0,), (0,)), ((), ())), precision=PRECISE)  1.76 us
    ppermute x1, starting transfers between devices, shards(): far_side = lax.ppermute(pair, 'ax', [(i, i ^ 2) for i in range(ax_count)])  1.44 us
    squeeze x2, local copies, waits for them, and re-layouts, shards(): lax.dynamic_index_in_dim(jnp.asarray(table, f32), circ_place, 0, False)  1.36 us
    dot_general x1, matrix products, shards(): ax_out = jnp.dot(rows, square, precision=PRECISE)  1.3 us
  transfers between devices with their start and end apart: 11, of which 4 were waited for; matrix products, arithmetic and copies ran while one was open for 12% of the time, Pallas kernels for 3%

profile of v3, /device:TPU:8, one launch (start us, length us, event | category | flops | bytes accessed | tf_op | source)
XLA Modules:
  0.0 43.9 jit_solution(12929566616054759316)
XLA Ops:
  0.6 1.1 %totals.1 = (f32[4,24,256]{2,1,0:T(8,128)S(1)}, f32[24,8,256]{2,1,0:T(8,128)S(1)}) custom-call(f32[24,8,256]{2,1,0:T(8,128)} %bitcast.22), custom_call_target="tpu_custom_call" | custom-call | tf_op jit(solution)/shard_map/totals/pallas_call | solution.py:340
  1.7 1.6 %collective-permute-start.2 = (f32[4,24,256]{2,1,0:T(8,128)S(1)}, f32[4,24,256]{2,1,0:T(8,128)S(1)}, u32[]{:S(2)}, u32[]{:S(2)}) collective-permute-start(f32[4,24,256]{2,1,0:T(8,128)S(1)} %get-tuple-element.15), channel_id=1, source_target_pairs={{0,4},{4,0},{8,12},{12,8},{16,20},{20,16},{24,28},{28,24},{32,36},... | collective-permute-start | bytes 294920 | tf_op jit(solution)/shard_map/ppermute | solution.py:355
  3.3 2.7 %collective-permute-start.3 = (f32[4,24,256]{2,1,0:T(8,128)S(1)}, f32[4,24,256]{2,1,0:T(8,128)S(1)}, u32[]{:S(2)}, u32[]{:S(2)}) collective-permute-start(f32[4,24,256]{2,1,0:T(8,128)S(1)} %get-tuple-element.15), channel_id=1, source_target_pairs={{0,8},{4,12},{8,0},{12,4},{16,24},{20,28},{24,16},{28,20},{32,40},... | collective-permute-start | bytes 294920 | tf_op jit(solution)/shard_map/ppermute | solution.py:355
  6.0 0.5 %collective-permute-start.4 = (f32[4,24,256]{2,1,0:T(8,128)S(1)}, f32[4,24,256]{2,1,0:T(8,128)S(1)}, u32[]{:S(2)}, u32[]{:S(2)}) collective-permute-start(f32[4,24,256]{2,1,0:T(8,128)S(1)} %get-tuple-element.15), channel_id=1, source_target_pairs={{0,12},{4,8},{8,4},{12,0},{16,28},{20,24},{24,20},{28,16},{32,44},... | collective-permute-start | bytes 294920 | tf_op jit(solution)/shard_map/ppermute | solution.py:355
  6.5 9.9 %collective-permute-start = (f32[24,4,256]{2,1,0:T(4,128)S(1)}, f32[24,4,256]{2,1,0:T(4,128)S(1)}, u32[]{:S(2)}, u32[]{:S(2)}) collective-permute-start(f32[24,4,256]{2,1,0:T(4,128)S(1)} %get-tuple-element.13), channel_id=1, source_target_pairs={{4,0},{8,4},{12,8},{16,12},{20,16},{24,20},{28,24},{32,28},{36,32}... | collective-permute-start | bytes 294920 | tf_op jit(solution)/shard_map/ppermute | solution.py:399
  16.4 0.0 collective-permute-start.1
  16.4 0.9 %fusion.2 = f32[4,192]{1,0:T(4,128)S(1)} fusion(f32[24,8,256]{2,1,0:T(8,128)S(1)} %get-tuple-element.12.u_ref, f32[4,4,256]{2,1,0:T(4,128)} %constant.79.clone, s32[]{:T(128)S(6)} %select_n.202), kind=kOutput, calls=%fused_computation.4 | convolution fusion | flops 2359296 | bytes 203780 | tf_op jit(solution)/shard_map/dot_general | solution.py:416
  17.3 0.0 collective-permute-done.2.refs_0_
  17.3 0.1 collective-permute-start.9
  17.5 0.1 collective-permute-start.5
  17.6 1.3 %convolution_bitcast_fusion = f32[192,256]{1,0:T(8,128)S(1)} fusion(f32[4,256,256]{2,1,0:T(8,128)} %constant.80.clone, s32[]{:T(128)S(6)} %select_n.202, f32[24,8,256]{2,1,0:T(8,128)S(1)} %get-tuple-element.12.u_ref), kind=kOutput, calls=%fused_computation | convolution fusion | flops 150994944 | bytes 655364 | tf_op jit(solution)/shard_map/dot_general | solution.py:421
  19.0 6.4 %collective-permute-done.5.refs_3_ = f32[4,24,256]{2,1,0:T(8,128)S(1)} collective-permute-done((f32[4,24,256]{2,1,0:T(8,128)S(1)}, f32[4,24,256]{2,1,0:T(8,128)S(1)}, u32[]{:S(2)}, u32[]{:S(2)}) %collective-permute-start.5) | collective-permute-done | bytes 98336 | tf_op jit(solution)/shard_map/ppermute | solution.py:372
  25.4 0.1 collective-permute-start.6
  25.5 0.7 %dynamic-slice_bitcast_fusion = f32[8,4]{0,1:T(4,128)S(1)} fusion(f32[64,8,4]{1,2,0:T(4,128)} %constant.78.clone, s32[]{:T(128)S(6)} %select_n.164), kind=kLoop, calls=%fused_computation.67 | loop fusion | bytes 260 | tf_op jit(solution)/shard_map/jit(dynamic_index_in_dim)/squeeze | solution.py:386
  26.2 0.7 %copy.8.coef_ref = f32[8,4]{1,0:T(8,128)} copy(f32[8,4]{0,1:T(4,128)S(1)} %dynamic-slice_bitcast_fusion) | data formatting | bytes 256 | tf_op jit(solution)/shard_map/jit(dynamic_index_in_dim)/squeeze | solution.py:386
  26.9 3.2 %collective-permute-done.6.refs_4_ = f32[4,24,256]{2,1,0:T(8,128)S(1)} collective-permute-done((f32[4,24,256]{2,1,0:T(8,128)S(1)}, f32[4,24,256]{2,1,0:T(8,128)S(1)}, u32[]{:S(2)}, u32[]{:S(2)}) %collective-permute-start.6) | collective-permute-done | bytes 98336 | tf_op jit(solution)/shard_map/ppermute | solution.py:372
  30.1 0.1 collective-permute-start.7
  30.3 1.4 %collective-permute-start.10 = (f32[8,192]{1,0:T(8,128)S(1)}, f32[8,192]{1,0:T(8,128)S(1)}, u32[]{:S(2)}, u32[]{:S(2)}) collective-permute-start(f32[8,192]{1,0:T(8,128)S(1)} %pad_maximum_fusion.4), channel_id=1, source_target_pairs={{0,2},{1,3},{2,0},{3,1},{4,6},{5,7},{6,4},{7,5},{8,10},{9,11},{10,... | collective-permute-start | bytes 18440 | tf_op jit(solution)/shard_map/ppermute | solution.py:419
  31.7 4.5 %collective-permute-done.7.refs_5_ = f32[4,24,256]{2,1,0:T(8,128)S(1)} collective-permute-done((f32[4,24,256]{2,1,0:T(8,128)S(1)}, f32[4,24,256]{2,1,0:T(8,128)S(1)}, u32[]{:S(2)}, u32[]{:S(2)}) %collective-permute-start.7) | collective-permute-done | bytes 98336 | tf_op jit(solution)/shard_map/ppermute | solution.py:372
  36.3 2.3 %collective-permute-start.8 = (f32[4,24,256]{2,1,0:T(8,128)S(1)}, f32[4,24,256]{2,1,0:T(8,128)S(1)}, u32[]{:S(2)}, u32[]{:S(2)}) collective-permute-start(f32[4,24,256]{2,1,0:T(8,128)S(1)} %pad_maximum_fusion.3.refs_6_), channel_id=1, source_target_pairs={{0,192},{4,196},{8,200},{12,204},{16,208},{20,212},{24,216},{28,22... | collective-permute-start | bytes 294920 | tf_op jit(solution)/shard_map/ppermute | solution.py:372
  38.6 1.8 %convolution_add_fusion = f32[192,256]{1,0:T(8,128)} fusion(f32[192,256]{1,0:T(8,128)S(1)} %convolution_bitcast_fusion, f32[8,192]{1,0:T(8,128)S(1)} %collective-permute-done.10, f32[4,192]{1,0:T(4,128)S(1)} %collective-permute-done.9, f32[4,12,256]{2,1,0:T(8,128)} %constant.81.clone, s32[]{:T(128)S(6)} %select_n.202), kind=kOutput, calls=%fused_computation.1 | convolution fusion | flops 7129344 | bytes 418820 | tf_op jit(solution)/shard_map/dot_general | solution.py:426
  40.3 1.3 %near.1 = (f32[24,8,256]{2,1,0:T(8,128)S(1)}, f32[24,8,256]{2,1,0:T(8,128)S(1)}, f32[4,8,256]{2,1,0:T(8,128)S(1)}) custom-call(f32[8,4]{1,0:T(8,128)} %copy.8.coef_ref, f32[24,8,256]{2,1,0:T(8,128)S(1)} %get-tuple-element.12.u_ref, f32[24,4,256]{2,1,0:T(4,128)S(1)} %collective-permute-done.right_ref, f32[24,4,256]{2,1,0:T(4,128)S(1)} %collective-permute-done.1.left_ref, ...), custom_call_target="tpu_custom_call" | custom-call | tf_op jit(solution)/shard_map/near/pallas_call | solution.py:404
  41.6 1.5 %collective-permute-done.8.got = f32[4,24,256]{2,1,0:T(8,128)S(1)} collective-permute-done((f32[4,24,256]{2,1,0:T(8,128)S(1)}, f32[4,24,256]{2,1,0:T(8,128)S(1)}, u32[]{:S(2)}, u32[]{:S(2)}) %collective-permute-start.8) | collective-permute-done | bytes 98336 | tf_op jit(solution)/shard_map/ppermute | solution.py:372
  43.1 0.8 %far.1 = (f32[24,8,256]{2,1,0:T(8,128)}, f32[24,8,256]{2,1,0:T(8,128)}) custom-call(f32[4,8,256]{2,1,0:T(8,128)S(1)} %get-tuple-element.16.tile_ref, f32[4,24,256]{2,1,0:T(8,128)S(1)} %collective-permute-done.8.got, f32[24,8,256]{2,1,0:T(8,128)S(1)} %get-tuple-element.17.d_near, f32[24,8,256]{2,1,0:T(8,128)S(1)} %get-tuple-element.18.f_near), custom_call_target="tpu_custom_call" | custom-call | tf_op jit(solution)/shard_map/far/pallas_call | solution.py:428
  (17 shorter events, 0.2 us)
Async XLA Ops:
  1.7 15.6 %collective-permute-start.2 = (f32[4,24,256]{2,1,0:T(8,128)S(1)}, f32[4,24,256]{2,1,0:T(8,128)S(1)}, u32[]{:S(2)}, u32[]{:S(2)}) collective-permute-start(f32[4,24,256]{2,1,0:T(8,128)S(1)} %get-tuple-element.15), channel_id=1, source_target_pairs={{0,4},{4,0},{8,12},{12,8},{16,20},{20,16},{24,28},{28,24},{32,36},... | collective-permute-start | bytes 294920 | tf_op jit(solution)/shard_map/ppermute | solution.py:355
  3.3 14.1 %collective-permute-start.3 = (f32[4,24,256]{2,1,0:T(8,128)S(1)}, f32[4,24,256]{2,1,0:T(8,128)S(1)}, u32[]{:S(2)}, u32[]{:S(2)}) collective-permute-start(f32[4,24,256]{2,1,0:T(8,128)S(1)} %get-tuple-element.15), channel_id=1, source_target_pairs={{0,8},{4,12},{8,0},{12,4},{16,24},{20,28},{24,16},{28,20},{32,40},... | collective-permute-start | bytes 294920 | tf_op jit(solution)/shard_map/ppermute | solution.py:355
  6.0 11.4 %collective-permute-start.4 = (f32[4,24,256]{2,1,0:T(8,128)S(1)}, f32[4,24,256]{2,1,0:T(8,128)S(1)}, u32[]{:S(2)}, u32[]{:S(2)}) collective-permute-start(f32[4,24,256]{2,1,0:T(8,128)S(1)} %get-tuple-element.15), channel_id=1, source_target_pairs={{0,12},{4,8},{8,4},{12,0},{16,28},{20,24},{24,20},{28,16},{32,44},... | collective-permute-start | bytes 294920 | tf_op jit(solution)/shard_map/ppermute | solution.py:355
  6.5 33.8 %collective-permute-start = (f32[24,4,256]{2,1,0:T(4,128)S(1)}, f32[24,4,256]{2,1,0:T(4,128)S(1)}, u32[]{:S(2)}, u32[]{:S(2)}) collective-permute-start(f32[24,4,256]{2,1,0:T(4,128)S(1)} %get-tuple-element.13), channel_id=1, source_target_pairs={{4,0},{8,4},{12,8},{16,12},{20,16},{24,20},{28,24},{32,28},{36,32}... | collective-permute-start | bytes 294920 | tf_op jit(solution)/shard_map/ppermute | solution.py:399
  16.4 24.0 %collective-permute-start.1 = (f32[24,4,256]{2,1,0:T(4,128)S(1)}, f32[24,4,256]{2,1,0:T(4,128)S(1)}, u32[]{:S(2)}, u32[]{:S(2)}) collective-permute-start(f32[24,4,256]{2,1,0:T(4,128)S(1)} %get-tuple-element.14), channel_id=1, source_target_pairs={{0,4},{4,8},{8,12},{12,16},{16,20},{20,24},{24,28},{28,32},{32,36}... | collective-permute-start | bytes 294920 | tf_op jit(solution)/shard_map/ppermute | solution.py:398
  17.3 12.9 %collective-permute-start.9 = (f32[4,192]{1,0:T(4,128)S(1)}, f32[4,192]{1,0:T(4,128)S(1)}, u32[]{:S(2)}, u32[]{:S(2)}) collective-permute-start(f32[4,192]{1,0:T(4,128)S(1)} %fusion.2), channel_id=1, source_target_pairs={{0,1},{1,0},{2,3},{3,2},{4,5},{5,4},{6,7},{7,6},{8,9},{9,8},{10,11... | collective-permute-start | bytes 9224 | tf_op jit(solution)/shard_map/ppermute | solution.py:417
  17.5 7.8 %collective-permute-start.5 = (f32[4,24,256]{2,1,0:T(8,128)S(1)}, f32[4,24,256]{2,1,0:T(8,128)S(1)}, u32[]{:S(2)}, u32[]{:S(2)}) collective-permute-start(f32[4,24,256]{2,1,0:T(8,128)S(1)} %pad_maximum_fusion), channel_id=1, source_target_pairs={{0,16},{4,20},{8,24},{12,28},{16,0},{20,4},{24,8},{28,12},{32,48},... | collective-permute-start | bytes 294920 | tf_op jit(solution)/shard_map/ppermute | solution.py:372
  25.4 4.7 %collective-permute-start.6 = (f32[4,24,256]{2,1,0:T(8,128)S(1)}, f32[4,24,256]{2,1,0:T(8,128)S(1)}, u32[]{:S(2)}, u32[]{:S(2)}) collective-permute-start(f32[4,24,256]{2,1,0:T(8,128)S(1)} %pad_maximum_fusion.1), channel_id=1, source_target_pairs={{0,32},{4,36},{8,40},{12,44},{16,48},{20,52},{24,56},{28,60},{32,0... | collective-permute-start | bytes 294920 | tf_op jit(solution)/shard_map/ppermute | solution.py:372
  30.1 6.1 %collective-permute-start.7 = (f32[4,24,256]{2,1,0:T(8,128)S(1)}, f32[4,24,256]{2,1,0:T(8,128)S(1)}, u32[]{:S(2)}, u32[]{:S(2)}) collective-permute-start(f32[4,24,256]{2,1,0:T(8,128)S(1)} %pad_maximum_fusion.2), channel_id=1, source_target_pairs={{0,64},{4,68},{8,72},{12,76},{16,80},{20,84},{24,88},{28,92},{32,9... | collective-permute-start | bytes 294920 | tf_op jit(solution)/shard_map/ppermute | solution.py:372
  30.3 8.3 %collective-permute-start.10 = (f32[8,192]{1,0:T(8,128)S(1)}, f32[8,192]{1,0:T(8,128)S(1)}, u32[]{:S(2)}, u32[]{:S(2)}) collective-permute-start(f32[8,192]{1,0:T(8,128)S(1)} %pad_maximum_fusion.4), channel_id=1, source_target_pairs={{0,2},{1,3},{2,0},{3,1},{4,6},{5,7},{6,4},{7,5},{8,10},{9,11},{10,... | collective-permute-start | bytes 18440 | tf_op jit(solution)/shard_map/ppermute | solution.py:419
  36.3 6.8 %collective-permute-start.8 = (f32[4,24,256]{2,1,0:T(8,128)S(1)}, f32[4,24,256]{2,1,0:T(8,128)S(1)}, u32[]{:S(2)}, u32[]{:S(2)}) collective-permute-start(f32[4,24,256]{2,1,0:T(8,128)S(1)} %pad_maximum_fusion.3.refs_6_), channel_id=1, source_target_pairs={{0,192},{4,196},{8,200},{12,204},{16,208},{20,212},{24,216},{28,22... | collective-permute-start | bytes 294920 | tf_op jit(solution)/shard_map/ppermute | solution.py:372

commit v4 on v3

--- a/solution.py
+++ b/solution.py
@@ -239,17 +239,18 @@
         last_ref[n] = un[cells - REACH :]
 
 
-def near_kernel(local, halo, count, roots, coef_ref, u_ref, right_ref, left_ref, *refs):
+def near_kernel(local, halo, count, roots, tile_ref, u_ref, right_ref, left_ref, *refs):
     got = refs[:count]
-    d_ref, f_ref, tile_ref, lr = refs[count:]
+    d_ref, f_ref, lr = refs[count:]
     lines, cells, width = u_ref.shape
     outs = (d_ref, f_ref)
     for v in range(4):
-        total = got[0][v] * coef_ref[0, v]
-        for k in range(1, count):
-            total = total + got[k][v] * coef_ref[k, v]
-        lr[v] = total
-        tile_ref[v] = jnp.full(tile_ref.shape[1:], coef_ref[count, v], jnp.float32)
+        for n in range(0, lines, 8):
+            part = slice(n, n + 8)
+            total = got[0][v, part] * tile_ref[v]
+            for k in range(1, count):
+                total = total + got[k][v, part] * tile_ref[4 * k + v]
+            lr[v, part] = total
     diag = {}
     for name, table in (("local", local), ("halo", halo)):
         for which in range(2):
@@ -294,7 +295,7 @@
     hbm = (d_hbm, f_hbm)
     for v in range(4):
         for n in range(0, lines, 8):
-            lr[v, n : n + 8] = got[v, n : n + 8] * tile_ref[v]
+            lr[v, n : n + 8] = got[v, n : n + 8] * tile_ref[tile_ref.shape[0] - 4 + v]
     copies = []
     for c in range(CHUNKS):
         part = pl.ds(c * chunk, chunk)
@@ -399,16 +400,17 @@
     right = lax.ppermute(first, "circ", gnir)
 
     local, halo = circ_tables(cells)
-    smem = [pl.BlockSpec(memory_space=pltpu.SMEM)]
+    tile = jnp.broadcast_to(coef.reshape(-1, 1, 1), (coef.size, 8, width))
+    tile = in_vmem(lax.optimization_barrier(tile))
     carries = [in_vmem(x) for x in got[:-1]]
-    d_near, f_near, tile = pl.pallas_call(
+    d_near, f_near = pl.pallas_call(
         functools.partial(near_kernel, local, halo, len(carries), roots),
-        out_shape=(pltpu.VMEM(u.shape, f32),) * 2 + (pltpu.VMEM((4, 8, width), f32),),
-        in_specs=smem + vmem(3 + len(carries)),
-        out_specs=tuple(vmem(3)),
+        out_shape=(pltpu.VMEM(u.shape, f32),) * 2,
+        in_specs=vmem(4 + len(carries)),
+        out_specs=tuple(vmem(2)),
         scratch_shapes=[pltpu.VMEM((4, lines, width), f32)],
         name="near",
-    )(coef, u_near, in_vmem(right), in_vmem(left), *carries)
+    )(tile, u_near, in_vmem(right), in_vmem(left), *carries)
 
     ax_local, ax_gather, ax_spread = axial_tables(width, ax_count)
     rows = u.reshape(lines * cells, width)
@@ -422,6 +424,7 @@
     order = np.asarray([[p ^ 1, p ^ 2, p ^ 3] for p in range(ax_count)])
     spread = np.stack([ax_spread[p][order[p]].reshape(12, width) for p in range(ax_count)])
     spread = lax.dynamic_index_in_dim(jnp.asarray(spread, f32), ax_place, 0, False)
+    spread = lax.optimization_barrier(spread)
     ax_in = jnp.concatenate([near_side, far_side], axis=0)
     ax_out = ax_out + lax.dot_general(ax_in, spread, (((0,), (0,)), ((), ())), precision=PRECISE)
 
@@ -436,7 +439,7 @@
             pltpu.SemaphoreType.DMA((2, CHUNKS)),
         ],
         name="far",
-    )(in_vmem(tile), in_vmem(got[-1]), in_vmem(d_near), in_vmem(f_near))
+    )(tile, in_vmem(got[-1]), in_vmem(d_near), in_vmem(f_near))
     shape = fields.shape
     return d_circ.reshape(shape), ax_out.reshape(shape), filtered.reshape(shape)
 

time: 44.2 us -> 47.9 us (1.084)
  the two profiles are of different devices: /device:TPU:8 before, /device:TPU:1 now
where the time goes in v4:
time: 47.9 us; the launch traced here: 47.7 us
  waiting for transfers between devices  21.4 us (45%)
  starting transfers between devices  18 us (38%)
  matrix products  3.24 us (7%)
  Pallas kernels  2.46 us (5%)
  local copies, waits for them, and re-layouts  1.6 us (3%)
  between operations  0.84 us (2%)
    ppermute x4, waiting for transfers between devices, shards(): lax.ppermute(totals, 'circ', [(i, i ^ masks[k]) for i in range(circ_count)])  21.4 us
    ppermute x1, starting transfers between devices, shards(): right = lax.ppermute(first, 'circ', gnir)  10.6 us
    ppermute x3, starting transfers between devices, shards(): lax.ppermute(totals, 'circ', [(i, i ^ m) for i in range(circ_count)])  4.61 us
    ppermute x1, starting transfers between devices, shards(): near_side = lax.ppermute(sent, 'ax', [(i, i ^ 1) for i in range(ax_count)])  1.88 us
    dot_general x1, matrix products, shards(): ax_out = jnp.dot(rows, square, precision=PRECISE)  1.29 us
    pallas_call x1, Pallas kernels, shards(): pl.pallas_call(functools.partial(totals_kernel, weights), out_shape=(pltp...  1.08 us
    dot_general x1, matrix products, shards(): lax.dot_general(ax_in, spread, (((0,), (0,)), ((), ())), precision=PRECISE)  1.05 us
  transfers between devices with their start and end apart: 11, of which 4 were waited for; matrix products, arithmetic and copies ran while one was open for 10% of the time, Pallas kernels for 1%

profile of v4, /device:TPU:1, one launch (start us, length us, event | category | flops | bytes accessed | tf_op | source)
XLA Modules:
  0.0 47.7 jit_solution(1277447131586399624)
XLA Ops:
  0.6 1.1 %totals.1 = (f32[4,24,256]{2,1,0:T(8,128)S(1)}, f32[24,8,256]{2,1,0:T(8,128)S(1)}) custom-call(f32[24,8,256]{2,1,0:T(8,128)} %bitcast.20), custom_call_target="tpu_custom_call" | custom-call | tf_op jit(solution)/shard_map/totals/pallas_call | solution.py:341
  1.7 2.1 %collective-permute-start = (f32[4,24,256]{2,1,0:T(8,128)S(1)}, f32[4,24,256]{2,1,0:T(8,128)S(1)}, u32[]{:S(2)}, u32[]{:S(2)}) collective-permute-start(f32[4,24,256]{2,1,0:T(8,128)S(1)} %get-tuple-element.11), channel_id=1, source_target_pairs={{0,4},{4,0},{8,12},{12,8},{16,20},{20,16},{24,28},{28,24},{32,36},... | collective-permute-start | bytes 294920 | tf_op jit(solution)/shard_map/ppermute | solution.py:356
  3.8 2.5 %collective-permute-start.1 = (f32[4,24,256]{2,1,0:T(8,128)S(1)}, f32[4,24,256]{2,1,0:T(8,128)S(1)}, u32[]{:S(2)}, u32[]{:S(2)}) collective-permute-start(f32[4,24,256]{2,1,0:T(8,128)S(1)} %get-tuple-element.11), channel_id=1, source_target_pairs={{0,8},{4,12},{8,0},{12,4},{16,24},{20,28},{24,16},{28,20},{32,40},... | collective-permute-start | bytes 294920 | tf_op jit(solution)/shard_map/ppermute | solution.py:356
  6.3 0.0 collective-permute-start.2
  6.3 10.6 %collective-permute-start.7 = (f32[24,4,256]{2,1,0:T(4,128)S(1)}, f32[24,4,256]{2,1,0:T(4,128)S(1)}, u32[]{:S(2)}, u32[]{:S(2)}) collective-permute-start(f32[24,4,256]{2,1,0:T(4,128)S(1)} %get-tuple-element.13), channel_id=1, source_target_pairs={{4,0},{8,4},{12,8},{16,12},{20,16},{24,20},{28,24},{32,28},{36,32}... | collective-permute-start | bytes 294920 | tf_op jit(solution)/shard_map/ppermute | solution.py:400
  17.0 1.3 %convolution_bitcast_fusion = f32[192,256]{1,0:T(8,128)S(1)} fusion(f32[4,256,256]{2,1,0:T(8,128)} %constant.80.clone, s32[]{:T(128)S(6)} %select_n.202, f32[24,8,256]{2,1,0:T(8,128)S(1)} %get-tuple-element.12.u_ref), kind=kOutput, calls=%fused_computation | convolution fusion | flops 150994944 | bytes 655364 | tf_op jit(solution)/shard_map/dot_general | solution.py:423
  18.3 0.9 %fusion.2 = f32[4,192]{1,0:T(4,128)S(1)} fusion(f32[24,8,256]{2,1,0:T(8,128)S(1)} %get-tuple-element.12.u_ref, f32[4,4,256]{2,1,0:T(4,128)} %constant.79.clone, s32[]{:T(128)S(6)} %select_n.202), kind=kOutput, calls=%fused_computation.4 | convolution fusion | flops 2359296 | bytes 203780 | tf_op jit(solution)/shard_map/dot_general | solution.py:418
  19.3 1.9 %collective-permute-start.9 = (f32[4,192]{1,0:T(4,128)S(1)}, f32[4,192]{1,0:T(4,128)S(1)}, u32[]{:S(2)}, u32[]{:S(2)}) collective-permute-start(f32[4,192]{1,0:T(4,128)S(1)} %fusion.2), channel_id=1, source_target_pairs={{0,1},{1,0},{2,3},{3,2},{4,5},{5,4},{6,7},{7,6},{8,9},{9,8},{10,11... | collective-permute-start | bytes 9224 | tf_op jit(solution)/shard_map/ppermute | solution.py:419
  21.2 0.1 collective-permute-start.3
  21.3 0.7 %constant_dynamic-slice_fusion = f32[1,8,4]{2,1,0:T(8,128)S(1)} fusion(f32[64,8,4]{2,1,0:T(8,128)} %constant.78.clone, s32[]{:T(128)S(6)} %select_n.164), kind=kLoop, calls=%fused_computation.68 | loop fusion | bytes 260 | tf_op jit(solution)/shard_map/jit(dynamic_index_in_dim)/dynamic_slice | solution.py:387
  22.0 0.1 broadcast_in_dim.7
  22.1 0.1 broadcast_in_dim.8.tile_ref
  22.2 7.4 %collective-permute-done.3.refs_3_ = f32[4,24,256]{2,1,0:T(8,128)S(1)} collective-permute-done((f32[4,24,256]{2,1,0:T(8,128)S(1)}, f32[4,24,256]{2,1,0:T(8,128)S(1)}, u32[]{:S(2)}, u32[]{:S(2)}) %collective-permute-start.3) | collective-permute-done | bytes 98336 | tf_op jit(solution)/shard_map/ppermute | solution.py:373
  29.6 0.1 collective-permute-start.4
  29.7 0.7 %dynamic-slice_bitcast_fusion = f32[12,256]{1,0:T(8,128)S(1)} fusion(f32[4,12,256]{2,1,0:T(8,128)} %constant.81.clone, s32[]{:T(128)S(6)} %select_n.202), kind=kLoop, calls=%fused_computation.62 | loop fusion | bytes 24580 | tf_op jit(solution)/shard_map/jit(dynamic_index_in_dim)/squeeze | solution.py:426
  30.4 3.2 %collective-permute-done.4.refs_4_ = f32[4,24,256]{2,1,0:T(8,128)S(1)} collective-permute-done((f32[4,24,256]{2,1,0:T(8,128)S(1)}, f32[4,24,256]{2,1,0:T(8,128)S(1)}, u32[]{:S(2)}, u32[]{:S(2)}) %collective-permute-start.4) | collective-permute-done | bytes 98336 | tf_op jit(solution)/shard_map/ppermute | solution.py:373
  33.7 0.1 collective-permute-start.5
  33.8 0.5 %collective-permute-start.10 = (f32[8,192]{1,0:T(8,128)S(1)}, f32[8,192]{1,0:T(8,128)S(1)}, u32[]{:S(2)}, u32[]{:S(2)}) collective-permute-start(f32[8,192]{1,0:T(8,128)S(1)} %pad_maximum_fusion.4), channel_id=1, source_target_pairs={{0,2},{1,3},{2,0},{3,1},{4,6},{5,7},{6,4},{7,5},{8,10},{9,11},{10,... | collective-permute-start | bytes 18440 | tf_op jit(solution)/shard_map/ppermute | solution.py:421
  34.3 6.9 %collective-permute-done.5.refs_5_ = f32[4,24,256]{2,1,0:T(8,128)S(1)} collective-permute-done((f32[4,24,256]{2,1,0:T(8,128)S(1)}, f32[4,24,256]{2,1,0:T(8,128)S(1)}, u32[]{:S(2)}, u32[]{:S(2)}) %collective-permute-start.5) | collective-permute-done | bytes 98336 | tf_op jit(solution)/shard_map/ppermute | solution.py:373
  41.2 0.1 collective-permute-start.6
  41.3 1.0 %convolution_add_fusion = f32[192,256]{1,0:T(8,128)} fusion(f32[192,256]{1,0:T(8,128)S(1)} %convolution_bitcast_fusion, f32[12,256]{1,0:T(8,128)S(1)} %dynamic-slice_bitcast_fusion, f32[8,192]{1,0:T(8,128)S(1)} %collective-permute-done.10, f32[4,192]{1,0:T(4,128)S(1)} %collective-permute-done.9), kind=kOutput, calls=%fused_computation.1 | convolution fusion | flops 7129344 | bytes 414720 | tf_op jit(solution)/shard_map/dot_general | solution.py:429
  42.3 0.6 %near.1 = (f32[24,8,256]{2,1,0:T(8,128)S(1)}, f32[24,8,256]{2,1,0:T(8,128)S(1)}) custom-call(f32[32,8,256]{2,1,0:T(8,128)S(1)} %broadcast_in_dim.8.tile_ref, f32[24,8,256]{2,1,0:T(8,128)S(1)} %get-tuple-element.12.u_ref, f32[24,4,256]{2,1,0:T(4,128)S(1)} %collective-permute-done.7.right_ref, f32[24,4,256]{2,1,0:T(4,128)S(1)} %collective-permute-done.8.left_ref, ...), custom_call_target="tpu_custom_call" | custom-call | tf_op jit(solution)/shard_map/near/pallas_call | solution.py:406
  42.9 3.9 %collective-permute-done.6.got = f32[4,24,256]{2,1,0:T(8,128)S(1)} collective-permute-done((f32[4,24,256]{2,1,0:T(8,128)S(1)}, f32[4,24,256]{2,1,0:T(8,128)S(1)}, u32[]{:S(2)}, u32[]{:S(2)}) %collective-permute-start.6) | collective-permute-done | bytes 98336 | tf_op jit(solution)/shard_map/ppermute | solution.py:373
  46.8 0.8 %far.1 = (f32[24,8,256]{2,1,0:T(8,128)}, f32[24,8,256]{2,1,0:T(8,128)}) custom-call(f32[32,8,256]{2,1,0:T(8,128)S(1)} %broadcast_in_dim.8.tile_ref, f32[4,24,256]{2,1,0:T(8,128)S(1)} %collective-permute-done.6.got, f32[24,8,256]{2,1,0:T(8,128)S(1)} %get-tuple-element.15.d_near, f32[24,8,256]{2,1,0:T(8,128)S(1)} %get-tuple-element.16.f_near), custom_call_target="tpu_custom_call" | custom-call | tf_op jit(solution)/shard_map/far/pallas_call | solution.py:431
  (19 shorter events, 0.2 us)
Async XLA Ops:
  1.7 17.5 %collective-permute-start = (f32[4,24,256]{2,1,0:T(8,128)S(1)}, f32[4,24,256]{2,1,0:T(8,128)S(1)}, u32[]{:S(2)}, u32[]{:S(2)}) collective-permute-start(f32[4,24,256]{2,1,0:T(8,128)S(1)} %get-tuple-element.11), channel_id=1, source_target_pairs={{0,4},{4,0},{8,12},{12,8},{16,20},{20,16},{24,28},{28,24},{32,36},... | collective-permute-start | bytes 294920 | tf_op jit(solution)/shard_map/ppermute | solution.py:356
  3.8 17.3 %collective-permute-start.1 = (f32[4,24,256]{2,1,0:T(8,128)S(1)}, f32[4,24,256]{2,1,0:T(8,128)S(1)}, u32[]{:S(2)}, u32[]{:S(2)}) collective-permute-start(f32[4,24,256]{2,1,0:T(8,128)S(1)} %get-tuple-element.11), channel_id=1, source_target_pairs={{0,8},{4,12},{8,0},{12,4},{16,24},{20,28},{24,16},{28,20},{32,40},... | collective-permute-start | bytes 294920 | tf_op jit(solution)/shard_map/ppermute | solution.py:356
  6.3 14.9 %collective-permute-start.2 = (f32[4,24,256]{2,1,0:T(8,128)S(1)}, f32[4,24,256]{2,1,0:T(8,128)S(1)}, u32[]{:S(2)}, u32[]{:S(2)}) collective-permute-start(f32[4,24,256]{2,1,0:T(8,128)S(1)} %get-tuple-element.11), channel_id=1, source_target_pairs={{0,12},{4,8},{8,4},{12,0},{16,28},{20,24},{24,20},{28,16},{32,44},... | collective-permute-start | bytes 294920 | tf_op jit(solution)/shard_map/ppermute | solution.py:356
  6.3 36.0 %collective-permute-start.7 = (f32[24,4,256]{2,1,0:T(4,128)S(1)}, f32[24,4,256]{2,1,0:T(4,128)S(1)}, u32[]{:S(2)}, u32[]{:S(2)}) collective-permute-start(f32[24,4,256]{2,1,0:T(4,128)S(1)} %get-tuple-element.13), channel_id=1, source_target_pairs={{4,0},{8,4},{12,8},{16,12},{20,16},{24,20},{28,24},{32,28},{36,32}... | collective-permute-start | bytes 294920 | tf_op jit(solution)/shard_map/ppermute | solution.py:400
  17.0 25.4 %collective-permute-start.8 = (f32[24,4,256]{2,1,0:T(4,128)S(1)}, f32[24,4,256]{2,1,0:T(4,128)S(1)}, u32[]{:S(2)}, u32[]{:S(2)}) collective-permute-start(f32[24,4,256]{2,1,0:T(4,128)S(1)} %get-tuple-element.14), channel_id=1, source_target_pairs={{0,4},{4,8},{8,12},{12,16},{16,20},{20,24},{24,28},{28,32},{32,36}... | collective-permute-start | bytes 294920 | tf_op jit(solution)/shard_map/ppermute | solution.py:399
  19.3 14.5 %collective-permute-start.9 = (f32[4,192]{1,0:T(4,128)S(1)}, f32[4,192]{1,0:T(4,128)S(1)}, u32[]{:S(2)}, u32[]{:S(2)}) collective-permute-start(f32[4,192]{1,0:T(4,128)S(1)} %fusion.2), channel_id=1, source_target_pairs={{0,1},{1,0},{2,3},{3,2},{4,5},{5,4},{6,7},{7,6},{8,9},{9,8},{10,11... | collective-permute-start | bytes 9224 | tf_op jit(solution)/shard_map/ppermute | solution.py:419
  21.2 8.4 %collective-permute-start.3 = (f32[4,24,256]{2,1,0:T(8,128)S(1)}, f32[4,24,256]{2,1,0:T(8,128)S(1)}, u32[]{:S(2)}, u32[]{:S(2)}) collective-permute-start(f32[4,24,256]{2,1,0:T(8,128)S(1)} %pad_maximum_fusion), channel_id=1, source_target_pairs={{0,16},{4,20},{8,24},{12,28},{16,0},{20,4},{24,8},{28,12},{32,48},... | collective-permute-start | bytes 294920 | tf_op jit(solution)/shard_map/ppermute | solution.py:373
  29.6 4.0 %collective-permute-start.4 = (f32[4,24,256]{2,1,0:T(8,128)S(1)}, f32[4,24,256]{2,1,0:T(8,128)S(1)}, u32[]{:S(2)}, u32[]{:S(2)}) collective-permute-start(f32[4,24,256]{2,1,0:T(8,128)S(1)} %pad_maximum_fusion.1), channel_id=1, source_target_pairs={{0,32},{4,36},{8,40},{12,44},{16,48},{20,52},{24,56},{28,60},{32,0... | collective-permute-start | bytes 294920 | tf_op jit(solution)/shard_map/ppermute | solution.py:373
  33.7 7.5 %collective-permute-start.5 = (f32[4,24,256]{2,1,0:T(8,128)S(1)}, f32[4,24,256]{2,1,0:T(8,128)S(1)}, u32[]{:S(2)}, u32[]{:S(2)}) collective-permute-start(f32[4,24,256]{2,1,0:T(8,128)S(1)} %pad_maximum_fusion.2), channel_id=1, source_target_pairs={{0,64},{4,68},{8,72},{12,76},{16,80},{20,84},{24,88},{28,92},{32,9... | collective-permute-start | bytes 294920 | tf_op jit(solution)/shard_map/ppermute | solution.py:373
  33.8 7.5 %collective-permute-start.10 = (f32[8,192]{1,0:T(8,128)S(1)}, f32[8,192]{1,0:T(8,128)S(1)}, u32[]{:S(2)}, u32[]{:S(2)}) collective-permute-start(f32[8,192]{1,0:T(8,128)S(1)} %pad_maximum_fusion.4), channel_id=1, source_target_pairs={{0,2},{1,3},{2,0},{3,1},{4,6},{5,7},{6,4},{7,5},{8,10},{9,11},{10,... | collective-permute-start | bytes 18440 | tf_op jit(solution)/shard_map/ppermute | solution.py:421
  41.2 5.7 %collective-permute-start.6 = (f32[4,24,256]{2,1,0:T(8,128)S(1)}, f32[4,24,256]{2,1,0:T(8,128)S(1)}, u32[]{:S(2)}, u32[]{:S(2)}) collective-permute-start(f32[4,24,256]{2,1,0:T(8,128)S(1)} %pad_maximum_fusion.3.refs_6_), channel_id=1, source_target_pairs={{0,192},{4,196},{8,200},{12,204},{16,208},{20,212},{24,216},{28,22... | collective-permute-start | bytes 294920 | tf_op jit(solution)/shard_map/ppermute | solution.py:373
